TPU v7x, 256 devices: a whole 4x4x8 slice. The times are simulated.
256 devices in a mesh: gx: 32 (over z_hi, y, core), gy: 8 (over z_lo, x).
Axes of the slice: x: 4, y: 4, z: 8 (z_hi: 4, z_lo: 2; z = z_hi * 2 + z_lo), core: 2. Of those that a mesh axis runs over, the one named last changes fastest.
Arguments:
- species: float32 [48, 256, 128, 128], P(None, 'gx', 'gy'), may hold values from 0.2 to 2
- rate_matrices: float32 [256, 128, 2304], P('gx', 'gy'), may hold values from -20 to 10, as said below
- loss_rates: float32 [48], replicated, may hold values from 0.05 to 0.5
- sweeps: int32 [256, 128], P('gx', 'gy'), may hold values from 5 to 10, as said below
- flow_rows: float32 [256, 128, 128], P('gx', 'gy'), may hold values from -0.24 to 0.24
- flow_columns: float32 [256, 128, 128], P('gx', 'gy'), may hold values from -0.24 to 0.24
Outputs:
- transported: float32 [48, 256, 128, 128], P(None, 'gx', 'gy')
Inputs may be any that keep to these rules, and one draw needn't show every extreme that they name: `rate_matrices`: each column's rate matrix times the time step, with a negative diagonal. Columns in rows 112 to 143 take 9 or 10 sweeps, all others 5 or 6; both 5 and 10 occur.
All inputs are finite; a program needn't handle non-finite values.
Results may differ from a plain program's by a relative error of at most 0.0003.
Values sent between devices are 32-bit elements; how exact they have to be, the bound alone decides.
No kernel may reach another device: no remote copies, remote signals or barrier semaphores. Data moves between devices by JAX's collectives and lax.ppermute only.
A program may use at most 128 MiB of HBM per device.

v0:
```python
import jax
import jax.numpy as jnp
from jax import lax
from jax.sharding import PartitionSpec as P

section_gamma = 1.0 + 0.5**0.5


def from_behind(array, axis, by):
    length = lax.axis_size(axis)
    pairs = [(i, i + by) for i in range(length) if 0 <= i + by < length]
    return lax.ppermute(array, axis, pairs)


def padded_2(array, sides, width):
    for axis, dim in sides:
        size, length = (lax.axis_size(axis), array.shape[dim])
        up = [(i, (i + 1) % size) for i in range(size - 1)]
        down = [(j, i) for i, j in up]
        last = lax.slice_in_dim(array, length - width, length, axis=dim)
        first = lax.slice_in_dim(array, 0, width, axis=dim)
        before = lax.ppermute(last, axis, up)
        after = lax.ppermute(first, axis, down)
        array = jnp.concatenate([before, array, after], axis=dim)
    return array


def linear_parts(matrices):
    species_count = matrices.shape[-1]
    identity = jnp.eye(species_count, dtype=jnp.float32)
    diagonal = jnp.sum(matrices * identity, axis=-1)
    coupling = section_gamma * (matrices * (1.0 - identity))
    scaled = 1.0 - section_gamma * diagonal
    return (coupling, scaled)


def product(matrices, values):
    return jnp.einsum("bij,bjn->bin", matrices, values, precision=lax.Precision.HIGHEST)


def tendency(matrices, values, loss_rates):
    return product(matrices, values) - loss_rates[:, None] * values * values


def advect(concentration, flow_first, flow_second):
    row_flux = (
        jnp.maximum(flow_first[:-1], 0.0) * concentration[:, :-1]
        + jnp.minimum(flow_first[:-1], 0.0) * concentration[:, 1:]
    )
    column_flux = (
        jnp.maximum(flow_second[:, :-1], 0.0) * concentration[:, :, :-1]
        + jnp.minimum(flow_second[:, :-1], 0.0) * concentration[:, :, 1:]
    )
    interior = concentration[:, 1:-1, 1:-1]
    return (
        interior
        - (row_flux[:, 1:, 1:-1] - row_flux[:, :-1, 1:-1])
        - (column_flux[:, 1:-1, 1:] - column_flux[:, 1:-1, :-1])
    )


def react_blocks(values, matrices, counts, loss_rates):
    coupling, scaled = linear_parts(matrices)
    trip_count = jnp.max(counts)

    def run_sweeps(source):

        def sweep_once(sweep_index, solved):
            update = (source + product(coupling, solved)) / scaled[:, :, None]
            return jnp.where((sweep_index < counts)[:, None, None], update, solved)

        return lax.fori_loop(0, trip_count, sweep_once, jnp.zeros_like(source))

    section_one = run_sweeps(tendency(matrices, values, loss_rates))
    shifted = values + section_one
    second = run_sweeps(tendency(matrices, shifted, loss_rates) - 2.0 * section_one)
    return values + 1.5 * section_one + 0.5 * second


def on_device(species, rate_matrices, loss_rates, sweeps, flow_rows, flow_columns):
    species_count, rows_here, columns_here, depth = species.shape
    block_count = rows_here * columns_here
    columns_first = jnp.transpose(species, (1, 2, 0, 3)).reshape(block_count, species_count, depth)
    matrices = rate_matrices.reshape(block_count, species_count, species_count)
    counts = sweeps.reshape(block_count)
    reacted = react_blocks(columns_first, matrices, counts, loss_rates)
    concentration = jnp.transpose(
        reacted.reshape(rows_here, columns_here, species_count, depth), (2, 0, 1, 3)
    )
    below_rows = from_behind(flow_rows[-1:], "gx", 1)
    below_columns = from_behind(flow_columns[:, -1:], "gy", 1)
    empty_row = jnp.zeros_like(below_rows)
    empty_column = jnp.zeros_like(below_columns)
    first_wide = jnp.concatenate([below_rows, flow_rows, empty_row], 0)
    first_wide = jnp.pad(first_wide, ((0, 0), (1, 1), (0, 0)))
    second_wide = jnp.concatenate([below_columns, flow_columns, empty_column], 1)
    second_wide = jnp.pad(second_wide, ((1, 1), (0, 0), (0, 0)))
    transported = concentration
    for substep in range(2):
        padded = padded_2(transported, (("gx", 1), ("gy", 2)), 1)
        transported = advect(padded, first_wide, second_wide)
    return transported


def solution(mesh):
    placed = (
        P(None, "gx", "gy", None),
        P("gx", "gy", None),
        P(),
        P("gx", "gy"),
        P("gx", "gy", None),
        P("gx", "gy", None),
    )
    return jax.shard_map(
        on_device, mesh=mesh, in_specs=placed, out_specs=P(None, "gx", "gy", None), check_vma=False
    )
```

profile of v0, /device:TPU:89, one launch (start us, length us, event | category | flops | bytes accessed | tf_op | source)
XLA Modules:
  0.0 278.6 jit_solution(13288063466718342579)
XLA Ops:
  3.8 4.6 %reshape.40 = f32[128,48,48]{2,1,0:T(8,128)} reshape(f32[8,16,2304]{2,1,0:T(8,128)} %param.11) | data formatting | bytes 2359296 | tf_op jit(solution)/shard_map/reshape | solution.py:84
  8.4 4.3 %multiply_reduce_fusion = (f32[128,48]{1,0:T(8,128)S(1)}, f32[128,48,48]{2,1,0:T(8,128)}) fusion(f32[128,48,48]{2,1,0:T(8,128)} %reshape.40, f32[48,48]{1,0:T(8,128)S(1)} %fusion.16, f32[48,48]{1,0:T(8,128)S(1)} %broadcast_subtract_fusion), kind=kLoop, calls=%fused_computation.32 | loop fusion | flops 1173504 | bytes 2402304 | tf_op jit(solution)/shard_map/reduce_sum | solution.py:31
  13.5 6.2 %fusion.4 = f32[128,48,128]{2,1,0:T(8,128)} fusion(f32[128,48,128]{2,1,0:T(8,128)S(1)} %bitcast.30, f32[128,48,48]{2,1,0:T(8,128)} %reshape.40, f32[48]{0:T(128)S(1)} %copy-done.8), kind=kOutput, calls=%fused_computation.20 | convolution fusion | flops 455344128 | bytes 7471296 | tf_op jit(solution)/shard_map/bij,bjn->bin/dot_general | solution.py:38
  19.9 75.2 %while.20 = (s32[]{:T(128)}, f32[128,48,128]{2,1,0:T(8,128)S(1)}, s32[]{:T(128)}, s32[128]{0:T(128)S(1)}, f32[128,48,48]{2,1,0:T(8,128)}, /*index=5*/f32[128,48,128]{2,1,0:T(8,128)}, f32[128,48]{1,0:T(8,128)S(1)}, s32[]{:T(128)}) while((s32[]{:T(128)}, f32[128,48,128]{2,1,0:T(8,128)S(1)}, s32[]{:T(128)}, s32[128]{0:T(128)S(1)}, ...), condition=%wide.region_3.4_spmd, body=%wide.region_2.3_spmd.sunk | while | flops 455344256 | bytes 34235280 | solution.py:72
  23.4 3.9 %divide_select_fusion.4 = f32[128,48,128]{2,1,0:T(8,128)S(1)} fusion(f32[128,48,128]{2,1,0:T(8,128)S(1)} %copy.30, f32[128,48,128]{2,1,0:T(8,128)S(1)} %copy-done.4, f32[128,48,48]{2,1,0:T(8,128)S(1)} %copy-done.1, f32[128,48]{1,0:T(8,128)S(1)} %get-tuple-element.235, pred[128]{0:T(512)(128)(4,1)S(1)} %broadcast_compare_fusion.4), kind=kOutput, calls=%fused_computation.clone.1 | convolution fusion | flops 455344128 | bytes 10641536 | tf_op jit(solution)/shard_map/while/body/bij,bjn->bin/dot_general | solution.py:38
  30.8 3.9 %divide_select_fusion.4 = f32[128,48,128]{2,1,0:T(8,128)S(1)} fusion(f32[128,48,128]{2,1,0:T(8,128)S(1)} %copy.30, f32[128,48,128]{2,1,0:T(8,128)S(1)} %copy-done.4, f32[128,48,48]{2,1,0:T(8,128)S(1)} %copy-done.1, f32[128,48]{1,0:T(8,128)S(1)} %get-tuple-element.235, pred[128]{0:T(512)(128)(4,1)S(1)} %broadcast_compare_fusion.4), kind=kOutput, calls=%fused_computation.clone.1 | convolution fusion | flops 455344128 | bytes 10641536 | tf_op jit(solution)/shard_map/while/body/bij,bjn->bin/dot_general | solution.py:38
  38.2 3.9 %divide_select_fusion.4 = f32[128,48,128]{2,1,0:T(8,128)S(1)} fusion(f32[128,48,128]{2,1,0:T(8,128)S(1)} %copy.30, f32[128,48,128]{2,1,0:T(8,128)S(1)} %copy-done.4, f32[128,48,48]{2,1,0:T(8,128)S(1)} %copy-done.1, f32[128,48]{1,0:T(8,128)S(1)} %get-tuple-element.235, pred[128]{0:T(512)(128)(4,1)S(1)} %broadcast_compare_fusion.4), kind=kOutput, calls=%fused_computation.clone.1 | convolution fusion | flops 455344128 | bytes 10641536 | tf_op jit(solution)/shard_map/while/body/bij,bjn->bin/dot_general | solution.py:38
  95.0 9.3 %fusion.6 = f32[128,48,128]{2,1,0:T(8,128)} fusion(f32[128,48,128]{2,1,0:T(8,128)S(1)} %get-tuple-element.81, f32[128,48,48]{2,1,0:T(8,128)} %reshape.40, f32[128,48,128]{2,1,0:T(8,128)} %bitcast.31, f32[48]{0:T(128)S(1)} %copy-done.8), kind=kOutput, calls=%fused_computation.22 | convolution fusion | flops 458489856 | bytes 10617024 | tf_op jit(solution)/shard_map/bij,bjn->bin/dot_general | solution.py:38
  106.2 95.7 %while.21 = (s32[]{:T(128)}, f32[128,48,128]{2,1,0:T(8,128)}, s32[]{:T(128)}, s32[128]{0:T(128)S(1)}, f32[128,48,48]{2,1,0:T(8,128)}, /*index=5*/f32[128,48,128]{2,1,0:T(8,128)}, f32[128,48]{1,0:T(8,128)S(1)}, s32[]{:T(128)}) while((s32[]{:T(128)}, f32[128,48,128]{2,1,0:T(8,128)}, s32[]{:T(128)}, s32[128]{0:T(128)S(1)}, ...), condition=%wide.region_5.6_spmd, body=%wide.region_4.5_spmd.sunk | while | flops 455344256 | bytes 34235280 | solution.py:72
  110.6 5.1 %divide_select_fusion.5 = f32[128,48,128]{2,1,0:T(8,128)} fusion(f32[128,48,128]{2,1,0:T(8,128)S(1)} %copy.31, f32[128,48,128]{2,1,0:T(8,128)S(1)} %copy-done.3, f32[128,48,48]{2,1,0:T(8,128)S(1)} %copy-done.2, f32[128,48]{1,0:T(8,128)S(1)} %get-tuple-element.259, pred[128]{0:T(512)(128)(4,1)S(1)} %broadcast_compare_fusion.5), kind=kOutput, calls=%fused_computation.2.clone.1 | convolution fusion | flops 455344128 | bytes 10641536 | tf_op jit(solution)/shard_map/while/body/bij,bjn->bin/dot_general | solution.py:38
  120.1 5.1 %divide_select_fusion.5 = f32[128,48,128]{2,1,0:T(8,128)} fusion(f32[128,48,128]{2,1,0:T(8,128)S(1)} %copy.31, f32[128,48,128]{2,1,0:T(8,128)S(1)} %copy-done.3, f32[128,48,48]{2,1,0:T(8,128)S(1)} %copy-done.2, f32[128,48]{1,0:T(8,128)S(1)} %get-tuple-element.259, pred[128]{0:T(512)(128)(4,1)S(1)} %broadcast_compare_fusion.5), kind=kOutput, calls=%fused_computation.2.clone.1 | convolution fusion | flops 455344128 | bytes 10641536 | tf_op jit(solution)/shard_map/while/body/bij,bjn->bin/dot_general | solution.py:38
  129.6 5.1 %divide_select_fusion.5 = f32[128,48,128]{2,1,0:T(8,128)} fusion(f32[128,48,128]{2,1,0:T(8,128)S(1)} %copy.31, f32[128,48,128]{2,1,0:T(8,128)S(1)} %copy-done.3, f32[128,48,48]{2,1,0:T(8,128)S(1)} %copy-done.2, f32[128,48]{1,0:T(8,128)S(1)} %get-tuple-element.259, pred[128]{0:T(512)(128)(4,1)S(1)} %broadcast_compare_fusion.5), kind=kOutput, calls=%fused_computation.2.clone.1 | convolution fusion | flops 455344128 | bytes 10641536 | tf_op jit(solution)/shard_map/while/body/bij,bjn->bin/dot_general | solution.py:38
  139.1 5.1 %divide_select_fusion.5 = f32[128,48,128]{2,1,0:T(8,128)} fusion(f32[128,48,128]{2,1,0:T(8,128)S(1)} %copy.31, f32[128,48,128]{2,1,0:T(8,128)S(1)} %copy-done.3, f32[128,48,48]{2,1,0:T(8,128)S(1)} %copy-done.2, f32[128,48]{1,0:T(8,128)S(1)} %get-tuple-element.259, pred[128]{0:T(512)(128)(4,1)S(1)} %broadcast_compare_fusion.5), kind=kOutput, calls=%fused_computation.2.clone.1 | convolution fusion | flops 455344128 | bytes 10641536 | tf_op jit(solution)/shard_map/while/body/bij,bjn->bin/dot_general | solution.py:38
  148.7 5.1 %divide_select_fusion.5 = f32[128,48,128]{2,1,0:T(8,128)} fusion(f32[128,48,128]{2,1,0:T(8,128)S(1)} %copy.31, f32[128,48,128]{2,1,0:T(8,128)S(1)} %copy-done.3, f32[128,48,48]{2,1,0:T(8,128)S(1)} %copy-done.2, f32[128,48]{1,0:T(8,128)S(1)} %get-tuple-element.259, pred[128]{0:T(512)(128)(4,1)S(1)} %broadcast_compare_fusion.5), kind=kOutput, calls=%fused_computation.2.clone.1 | convolution fusion | flops 455344128 | bytes 10641536 | tf_op jit(solution)/shard_map/while/body/bij,bjn->bin/dot_general | solution.py:38
  158.2 5.1 %divide_select_fusion.5 = f32[128,48,128]{2,1,0:T(8,128)} fusion(f32[128,48,128]{2,1,0:T(8,128)S(1)} %copy.31, f32[128,48,128]{2,1,0:T(8,128)S(1)} %copy-done.3, f32[128,48,48]{2,1,0:T(8,128)S(1)} %copy-done.2, f32[128,48]{1,0:T(8,128)S(1)} %get-tuple-element.259, pred[128]{0:T(512)(128)(4,1)S(1)} %broadcast_compare_fusion.5), kind=kOutput, calls=%fused_computation.2.clone.1 | convolution fusion | flops 455344128 | bytes 10641536 | tf_op jit(solution)/shard_map/while/body/bij,bjn->bin/dot_general | solution.py:38
  167.7 5.1 %divide_select_fusion.5 = f32[128,48,128]{2,1,0:T(8,128)} fusion(f32[128,48,128]{2,1,0:T(8,128)S(1)} %copy.31, f32[128,48,128]{2,1,0:T(8,128)S(1)} %copy-done.3, f32[128,48,48]{2,1,0:T(8,128)S(1)} %copy-done.2, f32[128,48]{1,0:T(8,128)S(1)} %get-tuple-element.259, pred[128]{0:T(512)(128)(4,1)S(1)} %broadcast_compare_fusion.5), kind=kOutput, calls=%fused_computation.2.clone.1 | convolution fusion | flops 455344128 | bytes 10641536 | tf_op jit(solution)/shard_map/while/body/bij,bjn->bin/dot_general | solution.py:38
  177.2 5.1 %divide_select_fusion.5 = f32[128,48,128]{2,1,0:T(8,128)} fusion(f32[128,48,128]{2,1,0:T(8,128)S(1)} %copy.31, f32[128,48,128]{2,1,0:T(8,128)S(1)} %copy-done.3, f32[128,48,48]{2,1,0:T(8,128)S(1)} %copy-done.2, f32[128,48]{1,0:T(8,128)S(1)} %get-tuple-element.259, pred[128]{0:T(512)(128)(4,1)S(1)} %broadcast_compare_fusion.5), kind=kOutput, calls=%fused_computation.2.clone.1 | convolution fusion | flops 455344128 | bytes 10641536 | tf_op jit(solution)/shard_map/while/body/bij,bjn->bin/dot_general | solution.py:38
  186.7 5.1 %divide_select_fusion.5 = f32[128,48,128]{2,1,0:T(8,128)} fusion(f32[128,48,128]{2,1,0:T(8,128)S(1)} %copy.31, f32[128,48,128]{2,1,0:T(8,128)S(1)} %copy-done.3, f32[128,48,48]{2,1,0:T(8,128)S(1)} %copy-done.2, f32[128,48]{1,0:T(8,128)S(1)} %get-tuple-element.259, pred[128]{0:T(512)(128)(4,1)S(1)} %broadcast_compare_fusion.5), kind=kOutput, calls=%fused_computation.2.clone.1 | convolution fusion | flops 455344128 | bytes 10641536 | tf_op jit(solution)/shard_map/while/body/bij,bjn->bin/dot_general | solution.py:38
  196.2 5.1 %divide_select_fusion.5 = f32[128,48,128]{2,1,0:T(8,128)} fusion(f32[128,48,128]{2,1,0:T(8,128)S(1)} %copy.31, f32[128,48,128]{2,1,0:T(8,128)S(1)} %copy-done.3, f32[128,48,48]{2,1,0:T(8,128)S(1)} %copy-done.2, f32[128,48]{1,0:T(8,128)S(1)} %get-tuple-element.259, pred[128]{0:T(512)(128)(4,1)S(1)} %broadcast_compare_fusion.5), kind=kOutput, calls=%fused_computation.2.clone.1 | convolution fusion | flops 455344128 | bytes 10641536 | tf_op jit(solution)/shard_map/while/body/bij,bjn->bin/dot_general | solution.py:38
  205.5 6.3 %collective-permute-start.1 = (f32[48,1,16,128]{3,0,2,1:T(8,128)S(1)}, f32[48,1,16,128]{3,0,2,1:T(8,128)S(1)}, u32[]{:S(2)}, u32[]{:S(2)}) collective-permute-start(f32[48,1,16,128]{3,0,2,1:T(8,128)S(1)} %get-tuple-element.117), channel_id=1, source_target_pairs={{0,8},{8,16},{16,24},{24,32},{32,40},{40,48},{48,56},{56,64},{64,7... | collective-permute-start | bytes 1179656 | tf_op jit(solution)/shard_map/ppermute | solution.py:22
  216.9 8.1 %collective-permute-start = (f32[1,16,128]{2,1,0:T(8,128)S(1)}, f32[1,16,128]{2,1,0:T(8,128)S(1)}, u32[]{:S(2)}, u32[]{:S(2)}) collective-permute-start(f32[1,16,128]{2,1,0:T(8,128)S(1)} %slice.86), channel_id=1, source_target_pairs={{0,8},{8,16},{16,24},{24,32},{32,40},{40,48},{48,56},{56,64},{64,7... | collective-permute-start | bytes 24584 | tf_op jit(solution)/shard_map/ppermute | solution.py:12
  225.3 4.0 %collective-permute-done.2 = f32[48,1,16,128]{3,0,2,1:T(8,128)S(1)} collective-permute-done((f32[48,1,16,128]{3,0,2,1:T(8,128)S(1)}, f32[48,1,16,128]{3,0,2,1:T(8,128)S(1)}, u32[]{:S(2)}, u32[]{:S(2)}) %collective-permute-start.2) | collective-permute-done | bytes 393248 | tf_op jit(solution)/shard_map/ppermute | solution.py:23
  235.6 4.1 %collective-permute-done.4 = f32[48,10,1,128]{3,0,2,1:T(8,128)S(1)} collective-permute-done((f32[48,10,1,128]{3,0,2,1:T(8,128)S(1)}, f32[48,10,1,128]{3,0,2,1:T(8,128)S(1)}, u32[]{:S(2)}, u32[]{:S(2)}) %collective-permute-start.4) | collective-permute-done | bytes 245792 | tf_op jit(solution)/shard_map/ppermute | solution.py:23
  250.8 12.5 %collective-permute-done.7 = f32[48,1,16,128]{3,0,2,1:T(8,128)S(1)} collective-permute-done((f32[48,1,16,128]{3,0,2,1:T(8,128)S(1)}, f32[48,1,16,128]{3,0,2,1:T(8,128)S(1)}, u32[]{:S(2)}, u32[]{:S(2)}) %collective-permute-start.7) | collective-permute-done | bytes 393248 | tf_op jit(solution)/shard_map/ppermute | solution.py:23
  (182 shorter events, 141.6 us)
Async XLA Ops:
  3.7 15.9 %copy-start = (f32[8,16,48,128]{3,2,1,0:T(8,128)}, f32[8,16,48,128]{3,2,1,0:T(8,128)S(1)}, u32[]{:S(2)}) copy-start(f32[8,16,48,128]{3,2,1,0:T(8,128)S(1)} %copy.11) | copy-start | bytes 9437188
  8.4 4.4 %copy-start.7 = (s32[8,16]{1,0:T(8,128)S(1)}, s32[8,16]{1,0:T(8,128)}, u32[]{:S(2)}) copy-start(s32[8,16]{1,0:T(8,128)} %param.13) | copy-start | bytes 1540
  8.4 5.1 %copy-start.8 = (f32[48]{0:T(128)S(1)}, f32[48]{0:T(128)}, u32[]{:S(2)}) copy-start(f32[48]{0:T(128)} %param.12) | copy-start | bytes 580
  106.8 3.8 %copy-start.3 = (f32[128,48,128]{2,1,0:T(8,128)S(1)}, f32[128,48,128]{2,1,0:T(8,128)}, u32[]{:S(2)}) copy-start(f32[128,48,128]{2,1,0:T(8,128)} %get-tuple-element.258) | copy-start | bytes 9437188 | tf_op jit(solution)/shard_map/while
  116.3 3.8 %copy-start.3 = (f32[128,48,128]{2,1,0:T(8,128)S(1)}, f32[128,48,128]{2,1,0:T(8,128)}, u32[]{:S(2)}) copy-start(f32[128,48,128]{2,1,0:T(8,128)} %get-tuple-element.258) | copy-start | bytes 9437188 | tf_op jit(solution)/shard_map/while
  125.9 3.8 %copy-start.3 = (f32[128,48,128]{2,1,0:T(8,128)S(1)}, f32[128,48,128]{2,1,0:T(8,128)}, u32[]{:S(2)}) copy-start(f32[128,48,128]{2,1,0:T(8,128)} %get-tuple-element.258) | copy-start | bytes 9437188 | tf_op jit(solution)/shard_map/while
  135.4 3.8 %copy-start.3 = (f32[128,48,128]{2,1,0:T(8,128)S(1)}, f32[128,48,128]{2,1,0:T(8,128)}, u32[]{:S(2)}) copy-start(f32[128,48,128]{2,1,0:T(8,128)} %get-tuple-element.258) | copy-start | bytes 9437188 | tf_op jit(solution)/shard_map/while
  144.9 3.8 %copy-start.3 = (f32[128,48,128]{2,1,0:T(8,128)S(1)}, f32[128,48,128]{2,1,0:T(8,128)}, u32[]{:S(2)}) copy-start(f32[128,48,128]{2,1,0:T(8,128)} %get-tuple-element.258) | copy-start | bytes 9437188 | tf_op jit(solution)/shard_map/while
  154.4 3.8 %copy-start.3 = (f32[128,48,128]{2,1,0:T(8,128)S(1)}, f32[128,48,128]{2,1,0:T(8,128)}, u32[]{:S(2)}) copy-start(f32[128,48,128]{2,1,0:T(8,128)} %get-tuple-element.258) | copy-start | bytes 9437188 | tf_op jit(solution)/shard_map/while
  163.9 3.8 %copy-start.3 = (f32[128,48,128]{2,1,0:T(8,128)S(1)}, f32[128,48,128]{2,1,0:T(8,128)}, u32[]{:S(2)}) copy-start(f32[128,48,128]{2,1,0:T(8,128)} %get-tuple-element.258) | copy-start | bytes 9437188 | tf_op jit(solution)/shard_map/while
  173.4 3.8 %copy-start.3 = (f32[128,48,128]{2,1,0:T(8,128)S(1)}, f32[128,48,128]{2,1,0:T(8,128)}, u32[]{:S(2)}) copy-start(f32[128,48,128]{2,1,0:T(8,128)} %get-tuple-element.258) | copy-start | bytes 9437188 | tf_op jit(solution)/shard_map/while
  192.4 3.8 %copy-start.3 = (f32[128,48,128]{2,1,0:T(8,128)S(1)}, f32[128,48,128]{2,1,0:T(8,128)}, u32[]{:S(2)}) copy-start(f32[128,48,128]{2,1,0:T(8,128)} %get-tuple-element.258) | copy-start | bytes 9437188 | tf_op jit(solution)/shard_map/while
  201.9 11.8 %copy-start.6 = (f32[8,16,128]{2,1,0:T(8,128)S(1)}, f32[8,16,128]{2,1,0:T(8,128)}, u32[]{:S(2)}) copy-start(f32[8,16,128]{2,1,0:T(8,128)} %param.15) | copy-start | bytes 196612
  201.9 15.0 %copy-start.5 = (f32[8,16,128]{2,1,0:T(8,128)S(1)}, f32[8,16,128]{2,1,0:T(8,128)}, u32[]{:S(2)}) copy-start(f32[8,16,128]{2,1,0:T(8,128)} %param.14) | copy-start | bytes 196612
  205.5 19.8 %collective-permute-start.1 = (f32[48,1,16,128]{3,0,2,1:T(8,128)S(1)}, f32[48,1,16,128]{3,0,2,1:T(8,128)S(1)}, u32[]{:S(2)}, u32[]{:S(2)}) collective-permute-start(f32[48,1,16,128]{3,0,2,1:T(8,128)S(1)} %get-tuple-element.117), channel_id=1, source_target_pairs={{0,8},{8,16},{16,24},{24,32},{32,40},{40,48},{48,56},{56,64},{64,7... | collective-permute-start | bytes 1179656 | tf_op jit(solution)/shard_map/ppermute | solution.py:22
  211.8 17.5 %collective-permute-start.2 = (f32[48,1,16,128]{3,0,2,1:T(8,128)S(1)}, f32[48,1,16,128]{3,0,2,1:T(8,128)S(1)}, u32[]{:S(2)}, u32[]{:S(2)}) collective-permute-start(f32[48,1,16,128]{3,0,2,1:T(8,128)S(1)} %get-tuple-element.118), channel_id=1, source_target_pairs={{8,0},{16,8},{24,16},{32,24},{40,32},{48,40},{56,48},{64,56},{72,6... | collective-permute-start | bytes 1179656 | tf_op jit(solution)/shard_map/ppermute | solution.py:23
  213.8 11.4 %collective-permute-start.5 = (f32[8,1,128]{2,1,0:T(1,128)S(1)}, f32[8,1,128]{2,1,0:T(1,128)S(1)}, u32[]{:S(2)}, u32[]{:S(2)}) collective-permute-start(f32[8,1,128]{2,1,0:T(1,128)S(1)} %slice.96), channel_id=1, source_target_pairs={{0,1},{1,2},{2,3},{3,4},{4,5},{5,6},{6,7},{8,9},{9,10},{10,11},{11... | collective-permute-start | bytes 12296 | tf_op jit(solution)/shard_map/ppermute | solution.py:12
  216.9 16.9 %collective-permute-start = (f32[1,16,128]{2,1,0:T(8,128)S(1)}, f32[1,16,128]{2,1,0:T(8,128)S(1)}, u32[]{:S(2)}, u32[]{:S(2)}) collective-permute-start(f32[1,16,128]{2,1,0:T(8,128)S(1)} %slice.86), channel_id=1, source_target_pairs={{0,8},{8,16},{16,24},{24,32},{32,40},{40,48},{48,56},{56,64},{64,7... | collective-permute-start | bytes 24584 | tf_op jit(solution)/shard_map/ppermute | solution.py:12
  229.4 6.2 %collective-permute-start.3 = (f32[48,10,1,128]{3,0,2,1:T(8,128)S(1)}, f32[48,10,1,128]{3,0,2,1:T(8,128)S(1)}, u32[]{:S(2)}, u32[]{:S(2)}) collective-permute-start(f32[48,10,1,128]{3,0,2,1:T(8,128)S(1)} %get-tuple-element.114), channel_id=1, source_target_pairs={{0,1},{1,2},{2,3},{3,4},{4,5},{5,6},{6,7},{8,9},{9,10},{10,11},{11... | collective-permute-start | bytes 737288 | tf_op jit(solution)/shard_map/ppermute | solution.py:22
  232.5 7.2 %collective-permute-start.4 = (f32[48,10,1,128]{3,0,2,1:T(8,128)S(1)}, f32[48,10,1,128]{3,0,2,1:T(8,128)S(1)}, u32[]{:S(2)}, u32[]{:S(2)}) collective-permute-start(f32[48,10,1,128]{3,0,2,1:T(8,128)S(1)} %get-tuple-element.113), channel_id=1, source_target_pairs={{1,0},{2,1},{3,2},{4,3},{5,4},{6,5},{7,6},{9,8},{10,9},{11,10},{12... | collective-permute-start | bytes 737288 | tf_op jit(solution)/shard_map/ppermute | solution.py:23
  243.1 7.6 %collective-permute-start.6 = (f32[48,1,16,128]{3,0,2,1:T(8,128)S(1)}, f32[48,1,16,128]{3,0,2,1:T(8,128)S(1)}, u32[]{:S(2)}, u32[]{:S(2)}) collective-permute-start(f32[48,1,16,128]{3,0,2,1:T(8,128)S(1)} %get-tuple-element.115), channel_id=1, source_target_pairs={{0,8},{8,16},{16,24},{24,32},{32,40},{40,48},{48,56},{56,64},{64,7... | collective-permute-start | bytes 1179656 | tf_op jit(solution)/shard_map/ppermute | solution.py:22
  246.0 17.2 %collective-permute-start.7 = (f32[48,1,16,128]{3,0,2,1:T(8,128)S(1)}, f32[48,1,16,128]{3,0,2,1:T(8,128)S(1)}, u32[]{:S(2)}, u32[]{:S(2)}) collective-permute-start(f32[48,1,16,128]{3,0,2,1:T(8,128)S(1)} %get-tuple-element.116), channel_id=1, source_target_pairs={{8,0},{16,8},{24,16},{32,24},{40,32},{48,40},{56,48},{64,56},{72,6... | collective-permute-start | bytes 1179656 | tf_op jit(solution)/shard_map/ppermute | solution.py:23
  263.3 5.3 %collective-permute-start.8 = (f32[48,10,1,128]{3,0,2,1:T(8,128)S(1)}, f32[48,10,1,128]{3,0,2,1:T(8,128)S(1)}, u32[]{:S(2)}, u32[]{:S(2)}) collective-permute-start(f32[48,10,1,128]{3,0,2,1:T(8,128)S(1)} %get-tuple-element.112), channel_id=1, source_target_pairs={{0,1},{1,2},{2,3},{3,4},{4,5},{5,6},{6,7},{8,9},{9,10},{10,11},{11... | collective-permute-start | bytes 737288 | tf_op jit(solution)/shard_map/ppermute | solution.py:22
  265.4 6.9 %collective-permute-start.9 = (f32[48,10,1,128]{3,0,2,1:T(8,128)S(1)}, f32[48,10,1,128]{3,0,2,1:T(8,128)S(1)}, u32[]{:S(2)}, u32[]{:S(2)}) collective-permute-start(f32[48,10,1,128]{3,0,2,1:T(8,128)S(1)} %get-tuple-element.111), channel_id=1, source_target_pairs={{1,0},{2,1},{3,2},{4,3},{5,4},{6,5},{7,6},{9,8},{10,9},{11,10},{12... | collective-permute-start | bytes 737288 | tf_op jit(solution)/shard_map/ppermute | solution.py:23
  (31 other events, 79.4 us)
where the time goes:
time: 279 us
  matrix products  106 us (38%)
  local copies, waits for them, and re-layouts  79.4 us (28%)
  starting transfers between devices  32.4 us (12%)
  waiting for transfers between devices  30.6 us (11%)
  other arithmetic  15.8 us (6%)
  loops' own time  14.6 us (5%)
    dot_general x22, matrix products, product(): jnp.einsum('bij,bjn->bin', matrices, values, precision=lax.Precision.HIGH...  106 us
    while x100, local copies, waits for them, and re-layouts  66 us
    ppermute x4, waiting for transfers between devices, padded_2(): after = lax.ppermute(first, axis, down)  24.4 us
    another operation x2, loops' own time, run_sweeps(): return lax.fori_loop(0, trip_count, sweep_once, jnp.zeros_like(source))  14.6 us
    ppermute x4, starting transfers between devices, padded_2(): before = lax.ppermute(last, axis, up)  14.5 us
    ppermute x2, starting transfers between devices, from_behind(): return lax.ppermute(array, axis, pairs)  11.3 us
    ppermute x4, starting transfers between devices, padded_2(): after = lax.ppermute(first, axis, down)  6.65 us
    ppermute x4, waiting for transfers between devices, padded_2(): before = lax.ppermute(last, axis, up)  6.1 us
  transfers between devices with their start and end apart: 10, of which 7 were waited for; matrix products, arithmetic and copies ran while one was open for 0% of the time, Pallas kernels for 0%

commit v1 on v0

v1 whole, which is shorter than its diff:
```python
import jax
import jax.numpy as jnp
from jax import lax
from jax.experimental import pallas as pl
from jax.experimental.pallas import tpu as pltpu
from jax.sharding import PartitionSpec as P

gamma = 1.0 + 0.5**0.5
species_count = 48
depth = 128
rows_here = 8
columns_here = 16
single = jnp.float32
half = jnp.bfloat16
vmem = 48 << 20


def left(matrix):
    high = matrix.astype(half).astype(single)
    first = (high + pltpu.roll(matrix - high, 64, 1)).astype(half)
    return jnp.concatenate([first, high.astype(half)[:, :species_count]], axis=1)


def right(values):
    high = values.astype(half)
    low = (values - high.astype(single)).astype(half)
    gap = jnp.zeros((16, values.shape[1]), half)
    return jnp.concatenate([high, gap, high, gap, low], axis=0)


def times(one, other):
    return jnp.dot(one, other, preferred_element_type=single)


def react_columns(loads, coefficients, loss, counts):
    every = range(len(loads))
    row = lax.broadcasted_iota(jnp.int32, (species_count, depth), 0)
    lane = lax.broadcasted_iota(jnp.int32, (species_count, depth), 1)
    eye = (row == lane).astype(single)
    inverse, one, left_one = [], [], []
    for c in every:
        matrix = coefficients[c]()
        scaled = 1.0 - gamma * jnp.sum(matrix * eye, axis=1, keepdims=True)
        inverse.append(1.0 / scaled)
        one.append((gamma * (matrix - matrix * eye)) * inverse[c])
        left_one.append(left(one[c]))
    two = [times(left_one[c], right(one[c])) for c in every]
    base = [times(left_one[c], right(loads[c]())) for c in every]
    left_two = [left(two[c]) for c in every]
    pair = [times(left_two[c], right(one[c] + pltpu.roll(two[c], 64, 1))) for c in every]
    three = [jnp.where(lane < species_count, pair[c], 0.0) for c in every]
    four = [jnp.where(lane < species_count, pltpu.roll(pair[c], 64, 1), 0.0) for c in every]
    five = [times(left_two[c], right(three[c])) for c in every]
    left_five = [left(five[c]) for c in every]
    rest = []
    for c in every:
        more = [(counts[c] > q).astype(single) for q in (5, 6, 7, 8, 9)]
        rest.append(
            eye * more[0] + one[c] * more[1] + two[c] * more[2] + three[c] * more[3] + four[c] * more[4]
        )
    high_part = [times(left_five[c], right(rest[c])) for c in every]
    left_sum = [left(eye + one[c] + two[c] + three[c] + four[c] + high_part[c]) for c in every]
    base = [(base[c] + (inverse[c] - 1.0) * loads[c]()) * (1.0 / gamma) for c in every]
    first = []
    for c in every:
        values = loads[c]()
        first.append(base[c] - (inverse[c] * loss) * (values * values))
    first = [times(left_sum[c], right(first[c])) for c in every]
    moved = [times(left_one[c], right(first[c])) for c in every]
    second = []
    for c in every:
        shifted = loads[c]() + first[c]
        second.append(
            base[c]
            + (moved[c] + (inverse[c] - 1.0) * first[c]) * (1.0 / gamma)
            - (inverse[c] * loss) * (shifted * shifted)
            - (2.0 * inverse[c]) * first[c]
        )
    second = [times(left_sum[c], right(second[c])) for c in every]
    return [loads[c]() + 1.5 * first[c] + 0.5 * second[c] for c in every]


def react_kernel(start, at_once, corner_row, counts_ref, x_ref, a_ref, loss_ref, fr_ref, fc_ref, o_ref, *rest):
    corner_ref, mats = rest if corner_row is not None else (None, rest[0])
    mats[...] = jnp.zeros_like(mats)
    for r in range(2):
        for h in range(2):
            for i in range(species_count):
                mats[r * 2 + h, 8 * i : 8 * i + 8, 0:species_count] = a_ref[
                    r, 8 * h : 8 * h + 8, species_count * i : species_count * i + species_count
                ]
    row = lax.broadcasted_iota(jnp.int32, (species_count, species_count), 0)
    lane = lax.broadcasted_iota(jnp.int32, (species_count, species_count), 1)
    loss = jnp.sum(jnp.where(row == lane, loss_ref[...], 0.0), axis=1, keepdims=True)
    flat = x_ref.reshape(species_count * 32, depth)
    for base in range(0, 32, at_once):
        span = range(base, base + at_once)
        results = react_columns(
            [(lambda c=c: flat[pl.ds(c, species_count, 32), :]) for c in span],
            [(lambda c=c: mats[c // 8, pl.ds(c % 8, species_count, 8), :]) for c in span],
            loss,
            [counts_ref[start + c // 16, c % 16] for c in span],
        )
        for c, result in zip(span, results):
            o_ref[c] = result
            if corner_row is not None and c // 16 == corner_row and c % 16 in (0, 15):
                corner_ref[(c % 16) // 15] = result
    if corner_row is not None:
        for k, ref in enumerate((fr_ref, fc_ref)):
            for r in range(2):
                o_ref[32 + k, 16 * r : 16 * r + 16, :] = ref[r]
            for e, column in enumerate((0, 15)):
                corner_ref[2, 8 * k + e : 8 * k + e + 1, :] = ref[corner_row, column : column + 1, :]


def react_rows(block, corner_row, species, matrices, loss, sweeps, flow_rows, flow_columns):
    total = 32 if corner_row is None else 34
    shapes = [jax.ShapeDtypeStruct((total, species_count, depth), single)]
    if corner_row is not None:
        shapes.append(jax.ShapeDtypeStruct((3, species_count, depth), single))
    spec = pltpu.PrefetchScalarGridSpec(
        num_scalar_prefetch=1,
        grid=(1,),
        in_specs=[
            pl.BlockSpec((species_count, 2, 16, depth), lambda g, _: (0, block, 0, 0)),
            pl.BlockSpec((2, 16, species_count**2), lambda g, _: (block, 0, 0)),
            pl.BlockSpec((1, species_count), lambda g, _: (0, 0)),
            pl.BlockSpec((2, 16, depth), lambda g, _: (block, 0, 0)),
            pl.BlockSpec((2, 16, depth), lambda g, _: (block, 0, 0)),
        ],
        out_specs=[pl.BlockSpec(s.shape, lambda g, _: (0, 0, 0)) for s in shapes],
        scratch_shapes=[pltpu.VMEM((4, 8 * species_count, depth), single)],
    )

    def body(*refs):
        react_kernel(2 * block, 16, corner_row, *refs)

    return pl.pallas_call(
        body,
        out_shape=shapes,
        grid_spec=spec,
        compiler_params=pltpu.CompilerParams(vmem_limit_bytes=vmem),
        name=f"react_{block}",
    )(sweeps, species, matrices, loss, flow_rows, flow_columns)


def pack_kernel(low, mid_a, mid_b, high, corner_up, corner_down, fr, fc, to_left, to_right, sems):
    copies = []

    def copy(source, target):
        k = len(copies)
        copies.append(pltpu.make_async_copy(source, target, sems.at[k]))
        copies[-1].start()

    for side, (target, column, corner) in enumerate(((to_left, 0, 0), (to_right, 14, 1))):
        for k, part in enumerate((low, mid_a, mid_b, high)):
            for r in range(2):
                first = 2 + (2 * k + r) * 2
                copy(part.at[pl.ds(16 * r + column, 2)], target.at[pl.ds(first, 2)])
        for first, part in ((0, corner_up), (18, corner_down)):
            copy(part.at[pl.ds(corner, 1)], target.at[pl.ds(first + corner, 1)])
    for side, (target, column, corner) in enumerate(((to_left, 0, 0), (to_right, 14, 1))):
        for k, flow in enumerate((fr, fc)):
            for r in range(8):
                first = 2 + 2 * r
                target[20 + k, first : first + 2, :] = flow[r, column : column + 2, :]
    for one in copies:
        one.wait()
    for side, (target, column, corner) in enumerate(((to_left, 0, 0), (to_right, 14, 1))):
        for k in range(2):
            for first, part in ((0, corner_up), (18, corner_down)):
                target[20 + k, first + corner : first + corner + 1, :] = part[
                    2, 8 * k + corner : 8 * k + corner + 1, :
                ]


def pack(low, mid_a, mid_b, high, corner_up, corner_down, flow_rows, flow_columns):
    inside = pl.BlockSpec(memory_space=pltpu.VMEM)
    outside = pl.BlockSpec(memory_space=pl.ANY)
    shape = jax.ShapeDtypeStruct((22, species_count, depth), single)
    return pl.pallas_call(
        pack_kernel,
        out_shape=[shape, shape],
        in_specs=[outside] * 4 + [inside] * 4,
        out_specs=[inside, inside],
        scratch_shapes=[pltpu.SemaphoreType.DMA((20,))],
        compiler_params=pltpu.CompilerParams(vmem_limit_bytes=vmem),
        name="pack",
    )(low, mid_a, mid_b, high, corner_up, corner_down, flow_rows, flow_columns)


def transport_kernel(
    inside_ref, low, mid_a, mid_b, high, above, below, before, after, fr_ref, fc_ref,
    o_ref, c, later, wide_rows, wide_columns, weights, extra, sems,
):
    g = pl.program_id(0)

    def step(source, target, r, columns, place):
        for j in columns:
            a = [weights[q, place, j : j + 1, :] for q in range(5)]
            yield j, (
                a[0] * source(0, j)
                + a[1] * source(-1, j)
                + a[2] * source(1, j)
                + a[3] * source(0, j - 1)
                + a[4] * source(0, j + 1)
            )

    def one_later(r):
        for j, value in step(lambda di, j: c[r + 1 + di, j + 1], later, r, range(18), r):
            later[r, j] = value

    @pl.when(g == 0)
    def _():
        copies = []

        def copy(source, target):
            k = len(copies)
            copies.append(pltpu.make_async_copy(source, target, sems.at[k]))
            copies[-1].start()

        for k, part in enumerate((above, low, mid_a, mid_b, high, below)):
            for r in range(2):
                copy(part.at[pl.ds(16 * r, 16)], c.at[2 * k + r, pl.ds(2, 16)])
        for part, column in ((before, 0), (after, 18)):
            for r in range(10):
                copy(part.at[pl.ds(2 * r, 2)], c.at[1 + r, pl.ds(column, 2)])
        for k, (part, start) in enumerate(((above, 32), (below, 32), (before, 20), (after, 20))):
            copy(part.at[pl.ds(start, 2)], extra.at[k])
        for one in copies:
            one.wait()
        for k, (wide, own) in enumerate(((wide_rows, fr_ref), (wide_columns, fc_ref))):
            wide[...] = jnp.zeros_like(wide)
            for r in range(8):
                wide[2 + r, 2:18, :] = own[r]
            for r in range(2):
                wide[r, 2:18, :] = extra[0, k, 16 * r : 16 * r + 16, :]
                wide[10 + r, 2:18, :] = extra[1, k, 16 * r : 16 * r + 16, :]
            for r in range(10):
                wide[1 + r, 0:2, :] = extra[2, k, 2 * r : 2 * r + 2, :]
                wide[1 + r, 18:20, :] = extra[3, k, 2 * r : 2 * r + 2, :]
        has = [inside_ref[q].astype(single) for q in range(4)]
        column = lax.broadcasted_iota(jnp.int32, (18, depth), 0)
        for r in range(10):
            rows_out, rows_in = wide_rows[r + 1, 1:19, :], wide_rows[r, 1:19, :]
            columns_out, columns_in = wide_columns[r + 1, 1:19, :], wide_columns[r + 1, 0:18, :]
            kept = jnp.where(column == 0, has[2], jnp.where(column == 17, has[3], 1.0))
            if r == 0:
                kept = kept * has[0]
            if r == 9:
                kept = kept * has[1]
            outward = (
                jnp.maximum(rows_out, 0.0)
                - jnp.minimum(rows_in, 0.0)
                + jnp.maximum(columns_out, 0.0)
                - jnp.minimum(columns_in, 0.0)
            )
            for q, weight in enumerate(
                (
                    1.0 - outward,
                    jnp.maximum(rows_in, 0.0),
                    -jnp.minimum(rows_out, 0.0),
                    jnp.maximum(columns_in, 0.0),
                    -jnp.minimum(columns_out, 0.0),
                )
            ):
                weights[q, r, 0:18, :] = kept * weight
        for r in range(10):
            one_later(r)


    flat = o_ref.reshape(species_count * 16, depth)
    for j, value in step(lambda di, j: later[g + 1 + di, j], o_ref, g, range(1, 17), g + 1):
        flat[pl.ds(j - 1, species_count, 16), :] = value


def transport(inside, low, mid_a, mid_b, high, above, below, before, after, flow_rows, flow_columns):
    outside = pl.BlockSpec(memory_space=pl.ANY)
    flow = pl.BlockSpec((8, 16, depth), lambda g, _: (0, 0, 0))
    spec = pltpu.PrefetchScalarGridSpec(
        num_scalar_prefetch=1,
        grid=(8,),
        in_specs=[outside] * 8 + [flow, flow],
        out_specs=pl.BlockSpec((species_count, 1, 16, depth), lambda g, _: (0, g, 0, 0)),
        scratch_shapes=[
            pltpu.VMEM((12, 20, species_count, depth), single),
            pltpu.VMEM((10, 18, species_count, depth), single),
            pltpu.VMEM((12, 24, depth), single),
            pltpu.VMEM((12, 24, depth), single),
            pltpu.VMEM((5, 10, 24, depth), single),
            pltpu.VMEM((4, 2, species_count, depth), single),
            pltpu.SemaphoreType.DMA((36,)),
        ],
    )
    return pl.pallas_call(
        transport_kernel,
        out_shape=jax.ShapeDtypeStruct((species_count, rows_here, columns_here, depth), single),
        grid_spec=spec,
        compiler_params=pltpu.CompilerParams(vmem_limit_bytes=vmem),
        name="transport",
    )(inside, low, mid_a, mid_b, high, above, below, before, after, flow_rows, flow_columns)


def onward(array, axis, by):
    length = lax.axis_size(axis)
    pairs = [(i, i + by) for i in range(length) if 0 <= i + by < length]
    return lax.ppermute(array, axis, pairs)


def on_device(species, rate_matrices, loss_rates, sweeps, flow_rows, flow_columns):
    loss = loss_rates.reshape(1, species_count)
    arguments = (species, rate_matrices, loss, sweeps, flow_rows, flow_columns)
    high, high_corner = react_rows(3, 1, *arguments)
    low, low_corner = react_rows(0, 0, *arguments)
    corner_up = onward(high_corner, "gx", 1)
    corner_down = onward(low_corner, "gx", -1)
    above = onward(high, "gx", 1)
    below = onward(low, "gx", -1)
    (mid_a,) = react_rows(1, None, *arguments)
    (mid_b,) = react_rows(2, None, *arguments)
    to_left, to_right = pack(low, mid_a, mid_b, high, corner_up, corner_down, flow_rows, flow_columns)
    before = onward(to_right, "gy", 1)
    after = onward(to_left, "gy", -1)
    x, y = lax.axis_index("gx"), lax.axis_index("gy")
    inside = jnp.stack(
        [x > 0, x < lax.axis_size("gx") - 1, y > 0, y < lax.axis_size("gy") - 1]
    ).astype(jnp.int32)
    return transport(inside, low, mid_a, mid_b, high, above, below, before, after, flow_rows, flow_columns)


def solution(mesh):
    placed = (
        P(None, "gx", "gy", None),
        P("gx", "gy", None),
        P(),
        P("gx", "gy"),
        P("gx", "gy", None),
        P("gx", "gy", None),
    )
    return jax.shard_map(
        on_device, mesh=mesh, in_specs=placed, out_specs=P(None, "gx", "gy", None), check_vma=False
    )
```

time: 279 us -> 80.3 us (0.29)
  the two profiles are of different devices: /device:TPU:89 before, /device:TPU:95 now
where the time goes in v1:
time: 80.3 us; the launch traced here: 79.8 us
  Pallas kernels  35.1 us (44%)
  starting transfers between devices  23.5 us (29%)
  waiting for transfers between devices  14.7 us (18%)
  local copies, waits for them, and re-layouts  6.19 us (8%)
    ppermute x6, starting transfers between devices, onward(): return lax.ppermute(array, axis, pairs)  23.5 us
    pallas_call x4, Pallas kernels, react_rows(): pl.pallas_call(body, out_shape=shapes, grid_spec=spec, compiler_params=pl...  23.3 us
    ppermute x6, waiting for transfers between devices, onward(): return lax.ppermute(array, axis, pairs)  14.7 us
    pallas_call x1, Pallas kernels, transport(): pl.pallas_call(transport_kernel, out_shape=jax.ShapeDtypeStruct((species_...  9.41 us
    unnamed x16, local copies, waits for them, and re-layouts  6.19 us
    pallas_call x1, Pallas kernels, pack(): pl.pallas_call(pack_kernel, out_shape=[shape, shape], in_specs=[outside]...  2.34 us
  transfers between devices with their start and end apart: 6, of which 3 were waited for; matrix products, arithmetic and copies ran while one was open for 0% of the time, Pallas kernels for 25%

profile of v1, /device:TPU:95, one launch (start us, length us, event | category | flops | bytes accessed | tf_op | source)
XLA Modules:
  0.0 79.8 jit_solution(15259341116994274877)
XLA Ops:
  0.0 1.9 %copy-done = f32[48,8,16,128]{3,2,1,0:T(8,128)S(1)} copy-done((f32[48,8,16,128]{3,2,1,0:T(8,128)S(1)}, f32[48,8,16,128]{3,2,1,0:T(8,128)}, u32[]{:S(2)}) %copy-start) | copy-done | bytes 3145752
  1.9 1.3 %copy-done.1 = f32[8,16,2304]{2,1,0:T(8,128)S(1)} copy-done((f32[8,16,2304]{2,1,0:T(8,128)S(1)}, f32[8,16,2304]{2,1,0:T(8,128)}, u32[]{:S(2)}) %copy-start.1) | copy-done | bytes 1179672
  3.2 0.8 %copy-done.2 = f32[8,16,128]{2,1,0:T(8,128)S(1)} copy-done((f32[8,16,128]{2,1,0:T(8,128)S(1)}, f32[8,16,128]{2,1,0:T(8,128)}, u32[]{:S(2)}) %copy-start.2) | copy-done | bytes 65560
  4.0 0.8 %copy-done.4 = f32[8,16,128]{2,1,0:T(8,128)S(1)} copy-done((f32[8,16,128]{2,1,0:T(8,128)S(1)}, f32[8,16,128]{2,1,0:T(8,128)}, u32[]{:S(2)}) %copy-start.4) | copy-done | bytes 65560
  4.8 0.7 copy-done.6
  5.5 0.7 copy-done.7
  6.2 5.8 %react_3.1 = (f32[34,48,128]{2,1,0:T(8,128)S(1)}, f32[3,48,128]{2,1,0:T(8,128)S(1)}) custom-call(s32[8,16]{1,0:T(8,128)S(1)} %copy-done.6, f32[48,8,16,128]{3,2,1,0:T(8,128)S(1)} %copy-done, f32[8,16,2304]{2,1,0:T(8,128)S(1)} %copy-done.1, f32[1,48]{1,0:T(1,128)S(1)} %bitcast.5, f32[8,16,128]{2,1,0:T(8,128)S(1)} %copy-done.2, f32[8,16,128]{2,1,0:T(8,128)S(1)} %copy-done.4), custom_call_target="tpu_custom_call" | custom-call | tf_op jit(solution)/shard_map/react_3/pallas_call | solution.py:138
  12.0 6.3 %collective-permute-start = (f32[34,48,128]{2,1,0:T(8,128)S(1)}, f32[34,48,128]{2,1,0:T(8,128)}, u32[]{:S(2)}, u32[]{:S(2)}) collective-permute-start(f32[34,48,128]{2,1,0:T(8,128)S(1)} %get-tuple-element.12.high), channel_id=1, source_target_pairs={{0,8},{8,16},{16,24},{24,32},{32,40},{40,48},{48,56},{56,64},{64,7... | collective-permute-start | bytes 2506760 | tf_op jit(solution)/shard_map/ppermute | solution.py:307
  18.4 5.8 %react_0.1 = (f32[34,48,128]{2,1,0:T(8,128)S(1)}, f32[3,48,128]{2,1,0:T(8,128)S(1)}) custom-call(s32[8,16]{1,0:T(8,128)S(1)} %copy-done.6, f32[48,8,16,128]{3,2,1,0:T(8,128)S(1)} %copy-done, f32[8,16,2304]{2,1,0:T(8,128)S(1)} %copy-done.1, f32[1,48]{1,0:T(1,128)S(1)} %bitcast.6, f32[8,16,128]{2,1,0:T(8,128)S(1)} %copy-done.2, f32[8,16,128]{2,1,0:T(8,128)S(1)} %copy-done.4), custom_call_target="tpu_custom_call" | custom-call | tf_op jit(solution)/shard_map/react_0/pallas_call | solution.py:138
  24.2 1.9 %collective-permute-start.1 = (f32[34,48,128]{2,1,0:T(8,128)S(1)}, f32[34,48,128]{2,1,0:T(8,128)}, u32[]{:S(2)}, u32[]{:S(2)}) collective-permute-start(f32[34,48,128]{2,1,0:T(8,128)S(1)} %get-tuple-element.11.low), channel_id=1, source_target_pairs={{8,0},{16,8},{24,16},{32,24},{40,32},{48,40},{56,48},{64,56},{72,6... | collective-permute-start | bytes 2506760 | tf_op jit(solution)/shard_map/ppermute | solution.py:307
  26.1 7.9 %collective-permute-start.2 = (f32[3,48,128]{2,1,0:T(8,128)S(1)}, f32[3,48,128]{2,1,0:T(8,128)S(1)}, u32[]{:S(2)}, u32[]{:S(2)}) collective-permute-start(f32[3,48,128]{2,1,0:T(8,128)S(1)} %get-tuple-element.13), channel_id=1, source_target_pairs={{0,8},{8,16},{16,24},{24,32},{32,40},{40,48},{48,56},{56,64},{64,7... | collective-permute-start | bytes 221192 | tf_op jit(solution)/shard_map/ppermute | solution.py:307
  34.0 2.1 %collective-permute-start.3 = (f32[3,48,128]{2,1,0:T(8,128)S(1)}, f32[3,48,128]{2,1,0:T(8,128)S(1)}, u32[]{:S(2)}, u32[]{:S(2)}) collective-permute-start(f32[3,48,128]{2,1,0:T(8,128)S(1)} %get-tuple-element.14), channel_id=1, source_target_pairs={{8,0},{16,8},{24,16},{32,24},{40,32},{48,40},{56,48},{64,56},{72,6... | collective-permute-start | bytes 221192 | tf_op jit(solution)/shard_map/ppermute | solution.py:307
  36.1 5.8 %react_2.1.mid_b = f32[32,48,128]{2,1,0:T(8,128)S(1)} custom-call(s32[8,16]{1,0:T(8,128)S(1)} %copy-done.6, f32[48,8,16,128]{3,2,1,0:T(8,128)S(1)} %copy-done, f32[8,16,2304]{2,1,0:T(8,128)S(1)} %copy-done.1, f32[1,48]{1,0:T(1,128)S(1)} %bitcast.7, f32[8,16,128]{2,1,0:T(8,128)S(1)} %copy-done.2, f32[8,16,128]{2,1,0:T(8,128)S(1)} %copy-done.4), custom_call_target="tpu_custom_call" | custom-call | tf_op jit(solution)/shard_map/react_2/pallas_call | solution.py:138
  41.9 0.0 copy-start.3
  41.9 0.0 copy-start.5
  42.0 5.8 %react_1.1.mid_a = f32[32,48,128]{2,1,0:T(8,128)S(1)} custom-call(s32[8,16]{1,0:T(8,128)S(1)} %copy-done.6, f32[48,8,16,128]{3,2,1,0:T(8,128)S(1)} %copy-done, f32[8,16,2304]{2,1,0:T(8,128)S(1)} %copy-done.1, f32[1,48]{1,0:T(1,128)S(1)} %bitcast.8, f32[8,16,128]{2,1,0:T(8,128)S(1)} %copy-done.2, f32[8,16,128]{2,1,0:T(8,128)S(1)} %copy-done.4), custom_call_target="tpu_custom_call" | custom-call | tf_op jit(solution)/shard_map/react_1/pallas_call | solution.py:138
  47.8 4.3 %collective-permute-done.3.corner_down = f32[3,48,128]{2,1,0:T(8,128)S(1)} collective-permute-done((f32[3,48,128]{2,1,0:T(8,128)S(1)}, f32[3,48,128]{2,1,0:T(8,128)S(1)}, u32[]{:S(2)}, u32[]{:S(2)}) %collective-permute-start.3) | collective-permute-done | bytes 73760 | tf_op jit(solution)/shard_map/ppermute | solution.py:307
  52.1 2.3 %pack.1 = (f32[22,48,128]{2,1,0:T(8,128)}, f32[22,48,128]{2,1,0:T(8,128)}) custom-call(f32[34,48,128]{2,1,0:T(8,128)S(1)} %get-tuple-element.11.low, f32[32,48,128]{2,1,0:T(8,128)S(1)} %react_1.1.mid_a, f32[32,48,128]{2,1,0:T(8,128)S(1)} %react_2.1.mid_b, f32[34,48,128]{2,1,0:T(8,128)S(1)} %get-tuple-element.12.high, ...), custom_call_target="tpu_custom_call" | custom-call | tf_op jit(solution)/shard_map/pack/pallas_call | solution.py:181
  54.4 3.3 %collective-permute-start.4 = (f32[22,48,128]{2,1,0:T(8,128)}, f32[22,48,128]{2,1,0:T(8,128)}, u32[]{:S(2)}, u32[]{:S(2)}) collective-permute-start(f32[22,48,128]{2,1,0:T(8,128)} %get-tuple-element.15), channel_id=1, source_target_pairs={{0,1},{1,2},{2,3},{3,4},{4,5},{5,6},{6,7},{8,9},{9,10},{10,11},{11... | collective-permute-start | bytes 1622024 | tf_op jit(solution)/shard_map/ppermute | solution.py:307
  57.7 2.0 %collective-permute-start.5 = (f32[22,48,128]{2,1,0:T(8,128)}, f32[22,48,128]{2,1,0:T(8,128)}, u32[]{:S(2)}, u32[]{:S(2)}) collective-permute-start(f32[22,48,128]{2,1,0:T(8,128)} %get-tuple-element.16), channel_id=1, source_target_pairs={{1,0},{2,1},{3,2},{4,3},{5,4},{6,5},{7,6},{9,8},{10,9},{11,10},{12... | collective-permute-start | bytes 1622024 | tf_op jit(solution)/shard_map/ppermute | solution.py:307
  59.8 0.1 add_convert_fusion.inside_ref
  59.8 5.0 %collective-permute-done.4.before = f32[22,48,128]{2,1,0:T(8,128)} collective-permute-done((f32[22,48,128]{2,1,0:T(8,128)}, f32[22,48,128]{2,1,0:T(8,128)}, u32[]{:S(2)}, u32[]{:S(2)}) %collective-permute-start.4) | collective-permute-done | bytes 540704 | tf_op jit(solution)/shard_map/ppermute | solution.py:307
  64.9 5.4 %collective-permute-done.5.after = f32[22,48,128]{2,1,0:T(8,128)} collective-permute-done((f32[22,48,128]{2,1,0:T(8,128)}, f32[22,48,128]{2,1,0:T(8,128)}, u32[]{:S(2)}, u32[]{:S(2)}) %collective-permute-start.5) | collective-permute-done | bytes 540704 | tf_op jit(solution)/shard_map/ppermute | solution.py:307
  70.3 9.4 %transport.1 = f32[48,8,16,128]{3,2,1,0:T(8,128)} custom-call(s32[4]{0:T(128)S(1)} %add_convert_fusion.inside_ref, f32[34,48,128]{2,1,0:T(8,128)S(1)} %get-tuple-element.11.low, f32[32,48,128]{2,1,0:T(8,128)S(1)} %react_1.1.mid_a, f32[32,48,128]{2,1,0:T(8,128)S(1)} %react_2.1.mid_b, f32[34,48,128]{2,1,0:T(8,128)S(1)} %get-tuple-element.12.high, ...), custom_call_target="tpu_custom_call" | custom-call | tf_op jit(solution)/shard_map/transport/pallas_call | solution.py:295
  (11 shorter events, 0.0 us)
Async XLA Ops:
  0.0 1.9 %copy-start = (f32[48,8,16,128]{3,2,1,0:T(8,128)S(1)}, f32[48,8,16,128]{3,2,1,0:T(8,128)}, u32[]{:S(2)}) copy-start(f32[48,8,16,128]{3,2,1,0:T(8,128)} %refs_1_.7) | copy-start | bytes 9437188
  1.9 1.3 %copy-start.1 = (f32[8,16,2304]{2,1,0:T(8,128)S(1)}, f32[8,16,2304]{2,1,0:T(8,128)}, u32[]{:S(2)}) copy-start(f32[8,16,2304]{2,1,0:T(8,128)} %refs_2_.7) | copy-start | bytes 3538948
  3.2 0.8 %copy-start.2 = (f32[8,16,128]{2,1,0:T(8,128)S(1)}, f32[8,16,128]{2,1,0:T(8,128)}, u32[]{:S(2)}) copy-start(f32[8,16,128]{2,1,0:T(8,128)} %fr_ref.1) | copy-start | bytes 196612
  4.0 0.8 %copy-start.4 = (f32[8,16,128]{2,1,0:T(8,128)S(1)}, f32[8,16,128]{2,1,0:T(8,128)}, u32[]{:S(2)}) copy-start(f32[8,16,128]{2,1,0:T(8,128)} %fc_ref.1) | copy-start | bytes 196612
  4.8 0.7 copy-start.6
  5.5 0.7 copy-start.7
  12.0 58.3 %collective-permute-start = (f32[34,48,128]{2,1,0:T(8,128)S(1)}, f32[34,48,128]{2,1,0:T(8,128)}, u32[]{:S(2)}, u32[]{:S(2)}) collective-permute-start(f32[34,48,128]{2,1,0:T(8,128)S(1)} %get-tuple-element.12.high), channel_id=1, source_target_pairs={{0,8},{8,16},{16,24},{24,32},{32,40},{40,48},{48,56},{56,64},{64,7... | collective-permute-start | bytes 2506760 | tf_op jit(solution)/shard_map/ppermute | solution.py:307
  24.2 46.1 %collective-permute-start.1 = (f32[34,48,128]{2,1,0:T(8,128)S(1)}, f32[34,48,128]{2,1,0:T(8,128)}, u32[]{:S(2)}, u32[]{:S(2)}) collective-permute-start(f32[34,48,128]{2,1,0:T(8,128)S(1)} %get-tuple-element.11.low), channel_id=1, source_target_pairs={{8,0},{16,8},{24,16},{32,24},{40,32},{48,40},{56,48},{64,56},{72,6... | collective-permute-start | bytes 2506760 | tf_op jit(solution)/shard_map/ppermute | solution.py:307
  26.1 21.7 %collective-permute-start.2 = (f32[3,48,128]{2,1,0:T(8,128)S(1)}, f32[3,48,128]{2,1,0:T(8,128)S(1)}, u32[]{:S(2)}, u32[]{:S(2)}) collective-permute-start(f32[3,48,128]{2,1,0:T(8,128)S(1)} %get-tuple-element.13), channel_id=1, source_target_pairs={{0,8},{8,16},{16,24},{24,32},{32,40},{40,48},{48,56},{56,64},{64,7... | collective-permute-start | bytes 221192 | tf_op jit(solution)/shard_map/ppermute | solution.py:307
  34.0 18.1 %collective-permute-start.3 = (f32[3,48,128]{2,1,0:T(8,128)S(1)}, f32[3,48,128]{2,1,0:T(8,128)S(1)}, u32[]{:S(2)}, u32[]{:S(2)}) collective-permute-start(f32[3,48,128]{2,1,0:T(8,128)S(1)} %get-tuple-element.14), channel_id=1, source_target_pairs={{8,0},{16,8},{24,16},{32,24},{40,32},{48,40},{56,48},{64,56},{72,6... | collective-permute-start | bytes 221192 | tf_op jit(solution)/shard_map/ppermute | solution.py:307
  41.9 10.2 %copy-start.3 = (f32[8,16,128]{2,1,0:T(8,128)S(1)}, f32[8,16,128]{2,1,0:T(8,128)}, u32[]{:S(2)}) copy-start(f32[8,16,128]{2,1,0:T(8,128)} %fr_ref.1) | copy-start | bytes 196612
  41.9 10.1 %copy-start.5 = (f32[8,16,128]{2,1,0:T(8,128)S(1)}, f32[8,16,128]{2,1,0:T(8,128)}, u32[]{:S(2)}) copy-start(f32[8,16,128]{2,1,0:T(8,128)} %fc_ref.1) | copy-start | bytes 196612
  54.4 10.4 %collective-permute-start.4 = (f32[22,48,128]{2,1,0:T(8,128)}, f32[22,48,128]{2,1,0:T(8,128)}, u32[]{:S(2)}, u32[]{:S(2)}) collective-permute-start(f32[22,48,128]{2,1,0:T(8,128)} %get-tuple-element.15), channel_id=1, source_target_pairs={{0,1},{1,2},{2,3},{3,4},{4,5},{5,6},{6,7},{8,9},{9,10},{10,11},{11... | collective-permute-start | bytes 1622024 | tf_op jit(solution)/shard_map/ppermute | solution.py:307
  57.7 12.5 %collective-permute-start.5 = (f32[22,48,128]{2,1,0:T(8,128)}, f32[22,48,128]{2,1,0:T(8,128)}, u32[]{:S(2)}, u32[]{:S(2)}) collective-permute-start(f32[22,48,128]{2,1,0:T(8,128)} %get-tuple-element.16), channel_id=1, source_target_pairs={{1,0},{2,1},{3,2},{4,3},{5,4},{6,5},{7,6},{9,8},{10,9},{11,10},{12... | collective-permute-start | bytes 1622024 | tf_op jit(solution)/shard_map/ppermute | solution.py:307

commit v2 on v1

v2 whole, which is shorter than its diff:
```python
import jax
import jax.numpy as jnp
from jax import lax
from jax.experimental import pallas as pl
from jax.experimental.pallas import tpu as pltpu
from jax.sharding import PartitionSpec as P

gamma = 1.0 + 0.5**0.5
species_count = 48
depth = 128
rows_here = 8
columns_here = 16
single = jnp.float32
half = jnp.bfloat16
vmem = 40 << 20
vmem_small = 16 << 20


def left(matrix):
    high = matrix.astype(half).astype(single)
    first = (high + pltpu.roll(matrix - high, 64, 1)).astype(half)
    return jnp.concatenate([first, high.astype(half)[:, :species_count]], axis=1)


def right(values):
    high = values.astype(half)
    low = (values - high.astype(single)).astype(half)
    gap = jnp.zeros((16, values.shape[1]), half)
    return jnp.concatenate([high, gap, high, gap, low], axis=0)


def times(one, other):
    return jnp.dot(one, other, preferred_element_type=single)


def react_columns(loads, coefficients, loss, counts):
    every = range(len(loads))
    row = lax.broadcasted_iota(jnp.int32, (species_count, depth), 0)
    lane = lax.broadcasted_iota(jnp.int32, (species_count, depth), 1)
    eye = (row == lane).astype(single)
    inverse, one, left_one = [], [], []
    for c in every:
        matrix = coefficients[c]()
        scaled = 1.0 - gamma * jnp.sum(matrix * eye, axis=1, keepdims=True)
        inverse.append(1.0 / scaled)
        one.append((gamma * (matrix - matrix * eye)) * inverse[c])
        left_one.append(left(one[c]))
    two = [times(left_one[c], right(one[c])) for c in every]
    base = [times(left_one[c], right(loads[c]())) for c in every]
    left_two = [left(two[c]) for c in every]
    pair = [times(left_two[c], right(one[c] + pltpu.roll(two[c], 64, 1))) for c in every]
    three = [jnp.where(lane < species_count, pair[c], 0.0) for c in every]
    four = [jnp.where(lane < species_count, pltpu.roll(pair[c], 64, 1), 0.0) for c in every]
    five = [times(left_two[c], right(three[c])) for c in every]
    left_five = [left(five[c]) for c in every]
    rest = []
    for c in every:
        more = [(counts[c] > q).astype(single) for q in (5, 6, 7, 8, 9)]
        rest.append(
            eye * more[0] + one[c] * more[1] + two[c] * more[2] + three[c] * more[3] + four[c] * more[4]
        )
    high_part = [times(left_five[c], right(rest[c])) for c in every]
    left_sum = [left(eye + one[c] + two[c] + three[c] + four[c] + high_part[c]) for c in every]
    base = [(base[c] + (inverse[c] - 1.0) * loads[c]()) * (1.0 / gamma) for c in every]
    first = []
    for c in every:
        values = loads[c]()
        first.append(base[c] - (inverse[c] * loss) * (values * values))
    first = [times(left_sum[c], right(first[c])) for c in every]
    moved = [times(left_one[c], right(first[c])) for c in every]
    second = []
    for c in every:
        shifted = loads[c]() + first[c]
        second.append(
            base[c]
            + (moved[c] + (inverse[c] - 1.0) * first[c]) * (1.0 / gamma)
            - (inverse[c] * loss) * (shifted * shifted)
            - (2.0 * inverse[c]) * first[c]
        )
    second = [times(left_sum[c], right(second[c])) for c in every]
    return [loads[c]() + 1.5 * first[c] + 0.5 * second[c] for c in every]


def react_kernel(first_row, rows, columns, at_once, counts_ref, x_ref, a_ref, loss_ref, mats, store):
    mats[...] = jnp.zeros_like(mats)
    total = len(rows)
    for r in range(total):
        for h in range(2):
            for i in range(species_count):
                mats[r * 2 + h, 8 * i : 8 * i + 8, 0:species_count] = a_ref[
                    r, 8 * h : 8 * h + 8, species_count * i : species_count * i + species_count
                ]
    row = lax.broadcasted_iota(jnp.int32, (species_count, species_count), 0)
    lane = lax.broadcasted_iota(jnp.int32, (species_count, species_count), 1)
    loss = jnp.sum(jnp.where(row == lane, loss_ref[...], 0.0), axis=1, keepdims=True)
    flat = x_ref.reshape(species_count * total * 16, depth)
    cells = [(r, y) for r in rows for y in columns]
    for start in range(0, len(cells), at_once):
        span = cells[start : start + at_once]
        results = react_columns(
            [(lambda r=r, y=y: flat[pl.ds(16 * r + y, species_count, 16 * total), :]) for r, y in span],
            [(lambda r=r, y=y: mats[2 * r + y // 8, pl.ds(y % 8, species_count, 8), :]) for r, y in span],
            loss,
            [counts_ref[first_row + r, y] for r, y in span],
        )
        for (r, y), result in zip(span, results):
            store(r, y, result)


def react_call(body, name, grid, rows, block, extra_specs, shapes, operands, limit=vmem):
    spec = pltpu.PrefetchScalarGridSpec(
        num_scalar_prefetch=1,
        grid=(grid,),
        in_specs=[
            pl.BlockSpec((species_count, rows, 16, depth), lambda g, _: (0, block(g), 0, 0)),
            pl.BlockSpec((rows, 16, species_count**2), lambda g, _: (block(g), 0, 0)),
            pl.BlockSpec((1, species_count), lambda g, _: (0, 0)),
            *extra_specs,
        ],
        out_specs=[pl.BlockSpec(s, lambda g, _: (0, 0, 0)) for s in shapes],
        scratch_shapes=[pltpu.VMEM((2 * rows, 8 * species_count, depth), single)],
    )
    return pl.pallas_call(
        body,
        out_shape=[jax.ShapeDtypeStruct(s, single) for s in shapes],
        grid_spec=spec,
        compiler_params=pltpu.CompilerParams(vmem_limit_bytes=limit),
        name=name,
    )(*operands)


def react_edges(species, matrices, loss, sweeps, flow_rows, flow_columns):
    def body(counts_ref, x_ref, a_ref, loss_ref, fr_ref, fc_ref, to_left, to_right, mats):
        g = pl.program_id(0)

        def store(r, y, result):
            target, column = (to_left, y) if y < 2 else (to_right, y - 14)
            target[2 * (4 * g + r) + column] = result

        react_kernel(4 * g, range(4), (0, 1, 14, 15), 16, counts_ref, x_ref, a_ref, loss_ref, mats, store)
        for target, column in ((to_left, 0), (to_right, 14)):
            for k, flow in enumerate((fr_ref, fc_ref)):
                for r in range(8):
                    target[16 + k, 2 * r : 2 * r + 2, :] = flow[r, column : column + 2, :]

    flow = pl.BlockSpec((8, 16, depth), lambda g, _: (0, 0, 0))
    shape = (18, species_count, depth)
    return react_call(
        body, "react_edges", 2, 4, lambda g: g, [flow, flow], [shape, shape],
        (sweeps, species, matrices, loss, flow_rows, flow_columns),
    )


def react_pair(pair, species, matrices, loss, sweeps, to_left, to_right):
    def body(counts_ref, x_ref, a_ref, loss_ref, left_ref, right_ref, o_ref, mats):
        def store(r, y, result):
            o_ref[16 * r + y] = result

        react_kernel(2 * pair, range(2), range(2, 14), 12, counts_ref, x_ref, a_ref, loss_ref, mats, store)
        for r in range(2):
            for y in range(2):
                o_ref[16 * r + y] = left_ref[2 * r + y]
                o_ref[16 * r + 14 + y] = right_ref[2 * r + y]

    edge = pl.BlockSpec((2 * 2, species_count, depth), lambda g, _: (pair, 0, 0))
    return react_call(
        body, f"react_pair_{pair}", 1, 2, lambda g: pair, [edge, edge], [(36, species_count, depth)],
        (sweeps, species, matrices, loss, to_left, to_right),
    )[0]


def react_middle(species, matrices, loss, sweeps):
    def body(counts_ref, x_ref, a_ref, loss_ref, o_ref, mats):
        g = pl.program_id(0)

        def store(r, y, result):
            o_ref[12 * (2 * g + r) + y - 2] = result

        react_kernel(2 + 2 * g, range(2), range(2, 14), 12, counts_ref, x_ref, a_ref, loss_ref, mats, store)

    return react_call(
        body, "react_middle", 2, 2, lambda g: 1 + g, [], [(48, species_count, depth)],
        (sweeps, species, matrices, loss),
    )[0]


def corner_kernel(low_in, high_in, before, after, fr_ref, fc_ref, low, high, flows, sems):
    copies = []

    def copy(source, target):
        k = len(copies)
        copies.append(pltpu.make_async_copy(source, target, sems.at[k]))
        copies[-1].start()

    for target, x in ((low, 0), (high, 7)):
        copy(before.at[pl.ds(2 * x + 1, 1)], target.at[pl.ds(32, 1)])
        copy(after.at[pl.ds(2 * x, 1)], target.at[pl.ds(33, 1)])
    flows[...] = jnp.zeros_like(flows)
    for t, (first, x) in enumerate(((0, 0), (6, 7))):
        for k, flow in enumerate((fr_ref, fc_ref)):
            for r in range(2):
                flows[t, k, 16 * r : 16 * r + 16, :] = flow[first + r]
            flows[t, k, 32:33, :] = before[16 + k, 2 * x + 1 : 2 * x + 2, :]
            flows[t, k, 33:34, :] = after[16 + k, 2 * x : 2 * x + 1, :]
    copy(flows.at[0], low.at[pl.ds(34, 2)])
    copy(flows.at[1], high.at[pl.ds(34, 2)])
    for one in copies:
        one.wait()


def add_corners(low, high, before, after, flow_rows, flow_columns):
    inside = pl.BlockSpec(memory_space=pltpu.VMEM)
    outside = pl.BlockSpec(memory_space=pl.ANY)
    shape = jax.ShapeDtypeStruct(low.shape, single)
    return pl.pallas_call(
        corner_kernel,
        out_shape=[shape, shape],
        in_specs=[outside, outside, inside, inside, inside, inside],
        out_specs=[outside, outside],
        input_output_aliases={0: 0, 1: 1},
        scratch_shapes=[pltpu.VMEM((2, 2, species_count, depth), single), pltpu.SemaphoreType.DMA((6,))],
        compiler_params=pltpu.CompilerParams(vmem_limit_bytes=vmem),
        name="add_corners",
    )(low, high, before, after, flow_rows, flow_columns)


def fill_weights(rows, has, weights, wide_rows, wide_columns):
    column = lax.broadcasted_iota(jnp.int32, (18, depth), 0)
    for i in rows:
        rows_out, rows_in = wide_rows[i + 2, 1:19, :], wide_rows[i + 1, 1:19, :]
        columns_out, columns_in = wide_columns[i + 2, 1:19, :], wide_columns[i + 2, 0:18, :]
        kept = jnp.where(column == 0, has[2], jnp.where(column == 17, has[3], 1.0))
        if i == -1:
            kept = kept * has[0]
        if i == 8:
            kept = kept * has[1]
        outward = (
            jnp.maximum(rows_out, 0.0)
            - jnp.minimum(rows_in, 0.0)
            + jnp.maximum(columns_out, 0.0)
            - jnp.minimum(columns_in, 0.0)
        )
        for q, weight in enumerate(
            (
                1.0 - outward,
                jnp.maximum(rows_in, 0.0),
                -jnp.minimum(rows_out, 0.0),
                jnp.maximum(columns_in, 0.0),
                -jnp.minimum(columns_out, 0.0),
            )
        ):
            weights[q, i + 1, 0:18, :] = kept * weight


def fill_inner(wide_rows, wide_columns, fr_ref, fc_ref, before, after):
    for k, (wide, own) in enumerate(((wide_rows, fr_ref), (wide_columns, fc_ref))):
        for r in range(8):
            wide[2 + r, 2:18, :] = own[r]
            wide[2 + r, 0:2, :] = before[16 + k, 2 * r : 2 * r + 2, :]
            wide[2 + r, 18:20, :] = after[16 + k, 2 * r : 2 * r + 2, :]


def move(source, weights, i, j):
    a = [weights[q, i + 1, j + 1 : j + 2, :] for q in range(5)]
    return (
        a[0] * source(i, j)
        + a[1] * source(i - 1, j)
        + a[2] * source(i + 1, j)
        + a[3] * source(i, j - 1)
        + a[4] * source(i, j + 1)
    )


def inner_kernel(
    inside_ref, low, middle, high, to_left, to_right, before, after, fr_ref, fc_ref,
    out, later, rows_out, wide_rows, wide_columns, weights, sems,
):
    fill_inner(wide_rows, wide_columns, fr_ref, fc_ref, before, after)
    fill_weights(range(1, 7), [inside_ref[q].astype(single) for q in range(4)], weights, wide_rows, wide_columns)

    def now(i, j):
        if j < 0:
            return before[2 * i + j + 2]
        if j > 15:
            return after[2 * i + j - 16]
        if i < 2:
            return low[16 * i + j]
        if i > 5:
            return high[16 * (i - 6) + j]
        if j < 2:
            return to_left[2 * i + j]
        if j > 13:
            return to_right[2 * i + j - 14]
        return middle[12 * (i - 2) + j - 2]

    copies = []
    for i in range(1, 7):
        for j in range(-1, 17):
            later[i - 1, j + 1] = move(now, weights, i, j)
        if i >= 3:
            x = i - 1
            flat = rows_out.at[x - 2].reshape(species_count * 16, depth)
            for j in range(16):
                flat[pl.ds(j, species_count, 16), :] = move(
                    lambda a, b: later[a - 1, b + 1], weights, x, j
                )
            copies.append(pltpu.make_async_copy(rows_out.at[x - 2], out.at[:, x], sems.at[x - 2]))
            copies[-1].start()
    for one in copies:
        one.wait()


def outer_kernel(
    inside_ref, done, inner, low, high, above, below, before, after, fr_ref, fc_ref,
    out, later, rows_out, wide_rows, wide_columns, weights, sems,
):
    fill_inner(wide_rows, wide_columns, fr_ref, fc_ref, before, after)
    for k, wide in enumerate((wide_rows, wide_columns)):
        for part, place in ((above, 0), (below, 10)):
            for r in range(2):
                wide[place + r, 2:18, :] = part[34 + k, 16 * r : 16 * r + 16, :]
        for part, place in ((above, 1), (below, 10)):
            wide[place, 1:2, :] = part[34 + k, 32:33, :]
            wide[place, 18:19, :] = part[34 + k, 33:34, :]
    rows = (-1, 0, 1, 6, 7, 8)
    fill_weights(rows, [inside_ref[q].astype(single) for q in range(4)], weights, wide_rows, wide_columns)

    def now(i, j):
        if i < 0 or i > 7:
            part, r = (above, i + 2) if i < 0 else (below, i - 8)
            if j < 0:
                return part[32]
            if j > 15:
                return part[33]
            return part[16 * r + j]
        if j < 0:
            return before[2 * i + j + 2]
        if j > 15:
            return after[2 * i + j - 16]
        return low[16 * i + j] if i < 2 else high[16 * (i - 6) + j]

    def soon(i, j):
        return inner[i - 1, j + 1] if 0 < i < 7 else later[{-1: 0, 0: 1, 7: 2, 8: 3}[i], j + 1]

    for q, i in enumerate((-1, 0, 7, 8)):
        for j in range(0, 16) if i in (-1, 8) else range(-1, 17):
            later[q, j + 1] = move(now, weights, i, j)
    copies = []
    for q, x in enumerate((0, 1, 6, 7)):
        flat = rows_out.at[q].reshape(species_count * 16, depth)
        for j in range(16):
            flat[pl.ds(j, species_count, 16), :] = move(soon, weights, x, j)
        copies.append(pltpu.make_async_copy(rows_out.at[q], out.at[:, x], sems.at[q]))
        copies[-1].start()
    for one in copies:
        one.wait()


def moved_call(body, name, inputs, shapes, specs, places, aliases):
    inside = pl.BlockSpec(memory_space=pltpu.VMEM)
    return pl.pallas_call(
        body,
        out_shape=shapes,
        in_specs=[pl.BlockSpec(memory_space=pltpu.SMEM)] + [
            pl.BlockSpec(memory_space=pl.ANY) if k in aliases else inside for k in range(1, len(inputs))
        ],
        out_specs=specs,
        input_output_aliases=aliases,
        scratch_shapes=[
            *places,
            pltpu.VMEM((4, species_count, 16, depth), single),
            pltpu.VMEM((12, 24, depth), single),
            pltpu.VMEM((12, 24, depth), single),
            pltpu.VMEM((5, 10, 24, depth), single),
            pltpu.SemaphoreType.DMA((4,)),
        ],
        compiler_params=pltpu.CompilerParams(vmem_limit_bytes=vmem_small),
        name=name,
    )(*inputs)


def transport(inside, low, middle, high, to_left, to_right, above, below, before, after, flow_rows, flow_columns):
    whole = jax.ShapeDtypeStruct((species_count, rows_here, columns_here, depth), single)
    outside = pl.BlockSpec(memory_space=pl.ANY)
    done, inner = moved_call(
        inner_kernel, "inner",
        (inside, low, middle, high, to_left, to_right, before, after, flow_rows, flow_columns),
        [whole, jax.ShapeDtypeStruct((6, 18, species_count, depth), single)],
        [outside, pl.BlockSpec(memory_space=pltpu.VMEM)], [], {},
    )
    return moved_call(
        outer_kernel, "outer",
        (inside, done, inner, low, high, above, below, before, after, flow_rows, flow_columns),
        whole, outside, [pltpu.VMEM((4, 18, species_count, depth), single)], {1: 0},
    )


def onward(array, axis, by):
    length = lax.axis_size(axis)
    pairs = [(i, i + by) for i in range(length) if 0 <= i + by < length]
    return lax.ppermute(array, axis, pairs)


def on_device(species, rate_matrices, loss_rates, sweeps, flow_rows, flow_columns):
    loss = loss_rates.reshape(1, species_count)
    arguments = (species, rate_matrices, loss, sweeps)
    kept = [pltpu.with_memory_space_constraint(a, pltpu.HBM) for a in (*arguments, flow_rows, flow_columns)]
    to_left, to_right = react_edges(*kept)
    before = onward(to_right, "gy", 1)
    after = onward(to_left, "gy", -1)
    high = react_pair(3, *arguments, to_left, to_right)
    low = react_pair(0, *arguments, to_left, to_right)
    low, high = add_corners(low, high, before, after, flow_rows, flow_columns)
    above = onward(high, "gx", 1)
    below = onward(low, "gx", -1)
    middle = react_middle(*arguments)
    x, y = lax.axis_index("gx"), lax.axis_index("gy")
    inside = jnp.stack(
        [x > 0, x < lax.axis_size("gx") - 1, y > 0, y < lax.axis_size("gy") - 1]
    ).astype(jnp.int32)
    return transport(
        inside, low, middle, high, to_left, to_right, above, below, before, after, flow_rows, flow_columns
    )


def solution(mesh):
    placed = (
        P(None, "gx", "gy", None),
        P("gx", "gy", None),
        P(),
        P("gx", "gy"),
        P("gx", "gy", None),
        P("gx", "gy", None),
    )
    return jax.shard_map(
        on_device, mesh=mesh, in_specs=placed, out_specs=P(None, "gx", "gy", None), check_vma=False
    )
```

time: 80.3 us -> 62.3 us (0.78)
  the two profiles are of different devices: /device:TPU:95 before, /device:TPU:198 now
where the time goes in v2:
time: 62.3 us; the launch traced here: 62 us
  Pallas kernels  35.8 us (57%)
  starting transfers between devices  14.7 us (24%)
  waiting for transfers between devices  7.88 us (13%)
  local copies, waits for them, and re-layouts  3.09 us (5%)
    pallas_call x4, Pallas kernels, react_call(): pl.pallas_call(body, out_shape=[jax.ShapeDtypeStruct(s, single) for s in...  28.4 us
    ppermute x4, starting transfers between devices, onward(): return lax.ppermute(array, axis, pairs)  14.7 us
    ppermute x4, waiting for transfers between devices, onward(): return lax.ppermute(array, axis, pairs)  7.88 us
    pallas_call x2, Pallas kernels, moved_call(): pl.pallas_call(body, out_shape=shapes, in_specs=[pl.BlockSpec(memory_spac...  7.02 us
    unnamed x28, local copies, waits for them, and re-layouts  3.09 us
  transfers between devices with their start and end apart: 4, of which 2 were waited for; matrix products, arithmetic and copies ran while one was open for 0% of the time, Pallas kernels for 36%

profile of v2, /device:TPU:198, one launch (start us, length us, event | category | flops | bytes accessed | tf_op | source)
XLA Modules:
  0.0 62.0 jit_solution(11822724247230312718)
XLA Ops:
  0.0 0.0 copy-start.13
  0.0 9.5 %react_edges.1 = (f32[18,48,128]{2,1,0:T(8,128)S(1)}, f32[18,48,128]{2,1,0:T(8,128)S(1)}) custom-call(s32[8,16]{1,0:T(8,128)} %counts_ref.7, f32[48,8,16,128]{3,2,1,0:T(8,128)} %x_ref.7, f32[8,16,2304]{2,1,0:T(8,128)} %a_ref.7, f32[1,48]{1,0:T(1,128)} %bitcast.5, f32[8,16,128]{2,1,0:T(8,128)} %fr_ref.7, f32[8,16,128]{2,1,0:T(8,128)} %fc_ref.7), custom_call_target="tpu_custom_call" | custom-call | tf_op jit(solution)/shard_map/react_edges/pallas_call | solution.py:123
  9.5 0.0 copy-start.2
  9.5 2.7 %collective-permute-start.1 = (f32[18,48,128]{2,1,0:T(8,128)S(1)}, f32[18,48,128]{2,1,0:T(8,128)S(1)}, u32[]{:S(2)}, u32[]{:S(2)}) collective-permute-start(f32[18,48,128]{2,1,0:T(8,128)S(1)} %get-tuple-element.11.left_ref.to_left), channel_id=1, source_target_pairs={{1,0},{2,1},{3,2},{4,3},{5,4},{6,5},{7,6},{9,8},{10,9},{11,10},{12... | collective-permute-start | bytes 1327112 | tf_op jit(solution)/shard_map/ppermute | solution.py:401
  12.3 5.2 %collective-permute-start = (f32[18,48,128]{2,1,0:T(8,128)S(1)}, f32[18,48,128]{2,1,0:T(8,128)S(1)}, u32[]{:S(2)}, u32[]{:S(2)}) collective-permute-start(f32[18,48,128]{2,1,0:T(8,128)S(1)} %get-tuple-element.12.right_ref.to_right), channel_id=1, source_target_pairs={{0,1},{1,2},{2,3},{3,4},{4,5},{5,6},{6,7},{8,9},{9,10},{10,11},{11... | collective-permute-start | bytes 1327112 | tf_op jit(solution)/shard_map/ppermute | solution.py:401
  17.5 4.8 %react_pair_3.1.high_in = f32[36,48,128]{2,1,0:T(8,128)S(1)} custom-call(s32[8,16]{1,0:T(8,128)S(1)} %copy-done.12, f32[48,8,16,128]{3,2,1,0:T(8,128)S(1)} %copy-done, f32[8,16,2304]{2,1,0:T(8,128)S(1)} %copy-done.1, f32[1,48]{1,0:T(1,128)S(1)} %bitcast.6, f32[18,48,128]{2,1,0:T(8,128)S(1)} %get-tuple-element.11.left_ref.to_left, ...), custom_call_target="tpu_custom_call" | custom-call | tf_op jit(solution)/shard_map/react_pair_3/pallas_call | solution.py:123
  22.4 0.0 copy-start.10
  22.4 0.0 copy-start.11
  22.4 4.8 %react_pair_0.1.low_in = f32[36,48,128]{2,1,0:T(8,128)S(1)} custom-call(s32[8,16]{1,0:T(8,128)S(1)} %copy-done.12, f32[48,8,16,128]{3,2,1,0:T(8,128)S(1)} %copy-done, f32[8,16,2304]{2,1,0:T(8,128)S(1)} %copy-done.1, f32[1,48]{1,0:T(1,128)S(1)} %bitcast.7, f32[18,48,128]{2,1,0:T(8,128)S(1)} %get-tuple-element.11.left_ref.to_left, ...), custom_call_target="tpu_custom_call" | custom-call | tf_op jit(solution)/shard_map/react_pair_0/pallas_call | solution.py:123
  27.3 0.0 collective-permute-done.1.after
  27.3 0.0 copy-start.4
  27.3 0.0 collective-permute-done.before
  27.3 0.3 add_corners.1
  27.7 4.7 %collective-permute-start.3 = (f32[36,48,128]{2,1,0:T(8,128)S(1)}, f32[36,48,128]{2,1,0:T(8,128)}, u32[]{:S(2)}, u32[]{:S(2)}) collective-permute-start(f32[36,48,128]{2,1,0:T(8,128)S(1)} %get-tuple-element.13.low), channel_id=1, source_target_pairs={{8,0},{16,8},{24,16},{32,24},{40,32},{48,40},{56,48},{64,56},{72,6... | collective-permute-start | bytes 2654216 | tf_op jit(solution)/shard_map/ppermute | solution.py:401
  32.4 2.1 %collective-permute-start.2 = (f32[36,48,128]{2,1,0:T(8,128)S(1)}, f32[36,48,128]{2,1,0:T(8,128)}, u32[]{:S(2)}, u32[]{:S(2)}) collective-permute-start(f32[36,48,128]{2,1,0:T(8,128)S(1)} %get-tuple-element.14.high), channel_id=1, source_target_pairs={{0,8},{8,16},{16,24},{24,32},{32,40},{40,48},{48,56},{56,64},{64,7... | collective-permute-start | bytes 2654216 | tf_op jit(solution)/shard_map/ppermute | solution.py:401
  34.5 9.3 %react_middle.1.middle = f32[48,48,128]{2,1,0:T(8,128)S(1)} custom-call(s32[8,16]{1,0:T(8,128)S(1)} %copy-done.12, f32[48,8,16,128]{3,2,1,0:T(8,128)S(1)} %copy-done, f32[8,16,2304]{2,1,0:T(8,128)S(1)} %copy-done.1, f32[1,48]{1,0:T(1,128)S(1)} %bitcast.8), custom_call_target="tpu_custom_call" | custom-call | tf_op jit(solution)/shard_map/react_middle/pallas_call | solution.py:123
  43.8 0.1 add_convert_fusion.inside_ref
  43.9 1.0 %copy-done.3 = f32[18,48,128]{2,1,0:T(8,128)S(1)} copy-done((f32[18,48,128]{2,1,0:T(8,128)S(1)}, f32[18,48,128]{2,1,0:T(8,128)}, u32[]{:S(2)}) %copy-start.3) | copy-done | bytes 442392
  44.9 1.0 %copy-done.5 = f32[18,48,128]{2,1,0:T(8,128)S(1)} copy-done((f32[18,48,128]{2,1,0:T(8,128)S(1)}, f32[18,48,128]{2,1,0:T(8,128)}, u32[]{:S(2)}) %copy-start.5) | copy-done | bytes 442392
  45.9 1.0 %copy-done.8 = f32[18,48,128]{2,1,0:T(8,128)S(1)} copy-done((f32[18,48,128]{2,1,0:T(8,128)S(1)}, f32[18,48,128]{2,1,0:T(8,128)}, u32[]{:S(2)}) %copy-start.8) | copy-done | bytes 442392
  46.9 3.2 %inner.1 = (f32[48,8,16,128]{3,2,1,0:T(8,128)}, f32[6,18,48,128]{3,2,1,0:T(8,128)S(1)}) custom-call(s32[4]{0:T(128)S(1)} %add_convert_fusion.inside_ref, f32[36,48,128]{2,1,0:T(8,128)S(1)} %get-tuple-element.13.low, f32[48,48,128]{2,1,0:T(8,128)S(1)} %react_middle.1.middle, f32[36,48,128]{2,1,0:T(8,128)S(1)} %get-tuple-element.14.high, ...), custom_call_target="tpu_custom_call" | custom-call | tf_op jit(solution)/shard_map/inner/pallas_call | solution.py:361
  50.1 0.6 collective-permute-done.3.below
  50.7 7.3 %collective-permute-done.2.above = f32[36,48,128]{2,1,0:T(8,128)} collective-permute-done((f32[36,48,128]{2,1,0:T(8,128)S(1)}, f32[36,48,128]{2,1,0:T(8,128)}, u32[]{:S(2)}, u32[]{:S(2)}) %collective-permute-start.2) | collective-permute-done | bytes 884768 | tf_op jit(solution)/shard_map/ppermute | solution.py:401
  58.0 3.8 %outer.1 = f32[48,8,16,128]{3,2,1,0:T(8,128)} custom-call(s32[4]{0:T(128)S(1)} %add_convert_fusion.inside_ref, f32[48,8,16,128]{3,2,1,0:T(8,128)} %get-tuple-element.15.done, f32[6,18,48,128]{3,2,1,0:T(8,128)S(1)} %get-tuple-element.16.inner, f32[36,48,128]{2,1,0:T(8,128)S(1)} %get-tuple-element.13.low, ...), custom_call_target="tpu_custom_call", output_to_operand_aliasing={{}: (1, {})} | custom-call | tf_op jit(solution)/shard_map/outer/pallas_call | solution.py:361
  (20 shorter events, 0.0 us)
Async XLA Ops:
  0.0 17.5 %copy-start.12 = (s32[8,16]{1,0:T(8,128)S(1)}, s32[8,16]{1,0:T(8,128)}, u32[]{:S(2)}) copy-start(s32[8,16]{1,0:T(8,128)} %counts_ref.7) | copy-start | bytes 1540
  0.0 17.5 %copy-start.1 = (f32[8,16,2304]{2,1,0:T(8,128)S(1)}, f32[8,16,2304]{2,1,0:T(8,128)}, u32[]{:S(2)}) copy-start(f32[8,16,2304]{2,1,0:T(8,128)} %a_ref.7) | copy-start | bytes 3538948
  0.0 17.5 %copy-start = (f32[48,8,16,128]{3,2,1,0:T(8,128)S(1)}, f32[48,8,16,128]{3,2,1,0:T(8,128)}, u32[]{:S(2)}) copy-start(f32[48,8,16,128]{3,2,1,0:T(8,128)} %x_ref.7) | copy-start | bytes 9437188
  0.0 17.5 %copy-start.13 = (f32[48]{0:T(128)S(1)}, f32[48]{0:T(128)}, u32[]{:S(2)}) copy-start(f32[48]{0:T(128)} %param.8) | copy-start | bytes 580
  9.5 17.7 %copy-start.2 = (f32[18,48,128]{2,1,0:T(8,128)}, f32[18,48,128]{2,1,0:T(8,128)S(1)}, u32[]{:S(2)}) copy-start(f32[18,48,128]{2,1,0:T(8,128)S(1)} %get-tuple-element.12.right_ref.to_right) | copy-start | bytes 1327108
  9.5 17.7 %collective-permute-start.1 = (f32[18,48,128]{2,1,0:T(8,128)S(1)}, f32[18,48,128]{2,1,0:T(8,128)S(1)}, u32[]{:S(2)}, u32[]{:S(2)}) collective-permute-start(f32[18,48,128]{2,1,0:T(8,128)S(1)} %get-tuple-element.11.left_ref.to_left), channel_id=1, source_target_pairs={{1,0},{2,1},{3,2},{4,3},{5,4},{6,5},{7,6},{9,8},{10,9},{11,10},{12... | collective-permute-start | bytes 1327112 | tf_op jit(solution)/shard_map/ppermute | solution.py:401
  12.3 15.0 %collective-permute-start = (f32[18,48,128]{2,1,0:T(8,128)S(1)}, f32[18,48,128]{2,1,0:T(8,128)S(1)}, u32[]{:S(2)}, u32[]{:S(2)}) collective-permute-start(f32[18,48,128]{2,1,0:T(8,128)S(1)} %get-tuple-element.12.right_ref.to_right), channel_id=1, source_target_pairs={{0,1},{1,2},{2,3},{3,4},{4,5},{5,6},{6,7},{8,9},{9,10},{10,11},{11... | collective-permute-start | bytes 1327112 | tf_op jit(solution)/shard_map/ppermute | solution.py:401
  22.4 4.9 %copy-start.10 = (f32[8,16,128]{2,1,0:T(8,128)S(1)}, f32[8,16,128]{2,1,0:T(8,128)}, u32[]{:S(2)}) copy-start(f32[8,16,128]{2,1,0:T(8,128)} %fr_ref.7) | copy-start | bytes 196612
  22.4 4.9 %copy-start.11 = (f32[8,16,128]{2,1,0:T(8,128)S(1)}, f32[8,16,128]{2,1,0:T(8,128)}, u32[]{:S(2)}) copy-start(f32[8,16,128]{2,1,0:T(8,128)} %fc_ref.7) | copy-start | bytes 196612
  27.3 7.2 %copy-start.4 = (f32[18,48,128]{2,1,0:T(8,128)}, f32[18,48,128]{2,1,0:T(8,128)S(1)}, u32[]{:S(2)}) copy-start(f32[18,48,128]{2,1,0:T(8,128)S(1)} %collective-permute-done.1.after) | copy-start | bytes 1327108
  27.3 7.2 %copy-start.7 = (f32[18,48,128]{2,1,0:T(8,128)}, f32[18,48,128]{2,1,0:T(8,128)S(1)}, u32[]{:S(2)}) copy-start(f32[18,48,128]{2,1,0:T(8,128)S(1)} %collective-permute-done.before) | copy-start | bytes 1327108
  27.7 23.0 %collective-permute-start.3 = (f32[36,48,128]{2,1,0:T(8,128)S(1)}, f32[36,48,128]{2,1,0:T(8,128)}, u32[]{:S(2)}, u32[]{:S(2)}) collective-permute-start(f32[36,48,128]{2,1,0:T(8,128)S(1)} %get-tuple-element.13.low), channel_id=1, source_target_pairs={{8,0},{16,8},{24,16},{32,24},{40,32},{48,40},{56,48},{64,56},{72,6... | collective-permute-start | bytes 2654216 | tf_op jit(solution)/shard_map/ppermute | solution.py:401
  32.4 25.6 %collective-permute-start.2 = (f32[36,48,128]{2,1,0:T(8,128)S(1)}, f32[36,48,128]{2,1,0:T(8,128)}, u32[]{:S(2)}, u32[]{:S(2)}) collective-permute-start(f32[36,48,128]{2,1,0:T(8,128)S(1)} %get-tuple-element.14.high), channel_id=1, source_target_pairs={{0,8},{8,16},{16,24},{24,32},{32,40},{40,48},{48,56},{56,64},{64,7... | collective-permute-start | bytes 2654216 | tf_op jit(solution)/shard_map/ppermute | solution.py:401
  43.9 1.0 %copy-start.3 = (f32[18,48,128]{2,1,0:T(8,128)S(1)}, f32[18,48,128]{2,1,0:T(8,128)}, u32[]{:S(2)}) copy-start(f32[18,48,128]{2,1,0:T(8,128)} %copy-done.2) | copy-start | bytes 1327108
  44.9 1.0 %copy-start.5 = (f32[18,48,128]{2,1,0:T(8,128)S(1)}, f32[18,48,128]{2,1,0:T(8,128)}, u32[]{:S(2)}) copy-start(f32[18,48,128]{2,1,0:T(8,128)} %copy-done.4) | copy-start | bytes 1327108
  45.9 1.0 %copy-start.8 = (f32[18,48,128]{2,1,0:T(8,128)S(1)}, f32[18,48,128]{2,1,0:T(8,128)}, u32[]{:S(2)}) copy-start(f32[18,48,128]{2,1,0:T(8,128)} %copy-done.7) | copy-start | bytes 1327108
  46.9 11.1 %copy-start.6 = (f32[18,48,128]{2,1,0:T(8,128)S(1)}, f32[18,48,128]{2,1,0:T(8,128)}, u32[]{:S(2)}) copy-start(f32[18,48,128]{2,1,0:T(8,128)} %copy-done.4) | copy-start | bytes 1327108
  46.9 11.1 %copy-start.9 = (f32[18,48,128]{2,1,0:T(8,128)S(1)}, f32[18,48,128]{2,1,0:T(8,128)}, u32[]{:S(2)}) copy-start(f32[18,48,128]{2,1,0:T(8,128)} %copy-done.7) | copy-start | bytes 1327108

commit v3 on v2

--- a/solution.py
+++ b/solution.py
@@ -18,15 +18,16 @@
 
 def left(matrix):
     high = matrix.astype(half).astype(single)
-    first = (high + pltpu.roll(matrix - high, 64, 1)).astype(half)
-    return jnp.concatenate([first, high.astype(half)[:, :species_count]], axis=1)
+    lane = lax.broadcasted_iota(jnp.int32, (species_count, depth), 1)
+    again = pltpu.roll(high, 96, 1)
+    first = jnp.where(lane < 96, high + pltpu.roll(matrix - high, 48, 1), again).astype(half)
+    return jnp.concatenate([first, again.astype(half)[:, :16]], axis=1)
 
 
 def right(values):
     high = values.astype(half)
     low = (values - high.astype(single)).astype(half)
-    gap = jnp.zeros((16, values.shape[1]), half)
-    return jnp.concatenate([high, gap, high, gap, low], axis=0)
+    return jnp.concatenate([high, high, low], axis=0)
 
 
 def times(one, other):
@@ -81,63 +82,71 @@
     return [loads[c]() + 1.5 * first[c] + 0.5 * second[c] for c in every]
 
 
-def react_kernel(first_row, rows, columns, at_once, counts_ref, x_ref, a_ref, loss_ref, mats, store):
+def react_kernel(parts, rows, columns, at_once, counts_ref, loss_ref, mats, store):
     mats[...] = jnp.zeros_like(mats)
     total = len(rows)
-    for r in range(total):
-        for h in range(2):
-            for i in range(species_count):
-                mats[r * 2 + h, 8 * i : 8 * i + 8, 0:species_count] = a_ref[
-                    r, 8 * h : 8 * h + 8, species_count * i : species_count * i + species_count
-                ]
+    for p, (_, _, a_ref) in enumerate(parts):
+        for r in range(total):
+            for h in range(2):
+                for i in range(species_count):
+                    mats[2 * (p * total + r) + h, 8 * i : 8 * i + 8, 0:species_count] = a_ref[
+                        r, 8 * h : 8 * h + 8, species_count * i : species_count * i + species_count
+                    ]
     row = lax.broadcasted_iota(jnp.int32, (species_count, species_count), 0)
     lane = lax.broadcasted_iota(jnp.int32, (species_count, species_count), 1)
     loss = jnp.sum(jnp.where(row == lane, loss_ref[...], 0.0), axis=1, keepdims=True)
-    flat = x_ref.reshape(species_count * total * 16, depth)
-    cells = [(r, y) for r in rows for y in columns]
+    flat = [x_ref.reshape(species_count * total * 16, depth) for _, x_ref, _ in parts]
+    cells = [(p, r, y) for p in range(len(parts)) for r in rows for y in columns]
     for start in range(0, len(cells), at_once):
         span = cells[start : start + at_once]
         results = react_columns(
-            [(lambda r=r, y=y: flat[pl.ds(16 * r + y, species_count, 16 * total), :]) for r, y in span],
-            [(lambda r=r, y=y: mats[2 * r + y // 8, pl.ds(y % 8, species_count, 8), :]) for r, y in span],
+            [
+                (lambda p=p, r=r, y=y: flat[p][pl.ds(16 * r + y, species_count, 16 * total), :])
+                for p, r, y in span
+            ],
+            [
+                (lambda p=p, r=r, y=y: mats[2 * (p * total + r) + y // 8, pl.ds(y % 8, species_count, 8), :])
+                for p, r, y in span
+            ],
             loss,
-            [counts_ref[first_row + r, y] for r, y in span],
-        )
-        for (r, y), result in zip(span, results):
-            store(r, y, result)
-
-
-def react_call(body, name, grid, rows, block, extra_specs, shapes, operands, limit=vmem):
+            [counts_ref[parts[p][0] + r, y] for p, r, y in span],
+        )
+        for (p, r, y), result in zip(span, results):
+            store(p, r, y, result)
+
+
+def react_call(body, name, grid, rows, blocks, extra_specs, shapes, operands):
+    parts = []
+    for block in blocks:
+        parts.append(pl.BlockSpec((species_count, rows, 16, depth), lambda g, _, b=block: (0, b(g), 0, 0)))
+        parts.append(pl.BlockSpec((rows, 16, species_count**2), lambda g, _, b=block: (b(g), 0, 0)))
     spec = pltpu.PrefetchScalarGridSpec(
         num_scalar_prefetch=1,
         grid=(grid,),
-        in_specs=[
-            pl.BlockSpec((species_count, rows, 16, depth), lambda g, _: (0, block(g), 0, 0)),
-            pl.BlockSpec((rows, 16, species_count**2), lambda g, _: (block(g), 0, 0)),
-            pl.BlockSpec((1, species_count), lambda g, _: (0, 0)),
-            *extra_specs,
-        ],
+        in_specs=[pl.BlockSpec((1, species_count), lambda g, _: (0, 0)), *parts, *extra_specs],
         out_specs=[pl.BlockSpec(s, lambda g, _: (0, 0, 0)) for s in shapes],
-        scratch_shapes=[pltpu.VMEM((2 * rows, 8 * species_count, depth), single)],
+        scratch_shapes=[pltpu.VMEM((2 * rows * len(blocks), 8 * species_count, depth), single)],
     )
     return pl.pallas_call(
         body,
         out_shape=[jax.ShapeDtypeStruct(s, single) for s in shapes],
         grid_spec=spec,
-        compiler_params=pltpu.CompilerParams(vmem_limit_bytes=limit),
+        compiler_params=pltpu.CompilerParams(vmem_limit_bytes=vmem),
         name=name,
     )(*operands)
 
 
 def react_edges(species, matrices, loss, sweeps, flow_rows, flow_columns):
-    def body(counts_ref, x_ref, a_ref, loss_ref, fr_ref, fc_ref, to_left, to_right, mats):
+    def body(counts_ref, loss_ref, x_ref, a_ref, fr_ref, fc_ref, to_left, to_right, mats):
         g = pl.program_id(0)
 
-        def store(r, y, result):
+        def store(_, r, y, result):
             target, column = (to_left, y) if y < 2 else (to_right, y - 14)
             target[2 * (4 * g + r) + column] = result
 
-        react_kernel(4 * g, range(4), (0, 1, 14, 15), 16, counts_ref, x_ref, a_ref, loss_ref, mats, store)
+        react_kernel(
+            [(4 * g, x_ref, a_ref)], range(4), (0, 1, 14, 15), 16, counts_ref, loss_ref, mats, store
+        )
         for target, column in ((to_left, 0), (to_right, 14)):
             for k, flow in enumerate((fr_ref, fc_ref)):
                 for r in range(8):
@@ -146,41 +155,50 @@
     flow = pl.BlockSpec((8, 16, depth), lambda g, _: (0, 0, 0))
     shape = (18, species_count, depth)
     return react_call(
-        body, "react_edges", 2, 4, lambda g: g, [flow, flow], [shape, shape],
-        (sweeps, species, matrices, loss, flow_rows, flow_columns),
-    )
-
-
-def react_pair(pair, species, matrices, loss, sweeps, to_left, to_right):
-    def body(counts_ref, x_ref, a_ref, loss_ref, left_ref, right_ref, o_ref, mats):
-        def store(r, y, result):
-            o_ref[16 * r + y] = result
-
-        react_kernel(2 * pair, range(2), range(2, 14), 12, counts_ref, x_ref, a_ref, loss_ref, mats, store)
-        for r in range(2):
-            for y in range(2):
-                o_ref[16 * r + y] = left_ref[2 * r + y]
-                o_ref[16 * r + 14 + y] = right_ref[2 * r + y]
-
-    edge = pl.BlockSpec((2 * 2, species_count, depth), lambda g, _: (pair, 0, 0))
+        body, "react_edges", 2, 4, [lambda g: g], [flow, flow], [shape, shape],
+        (sweeps, loss, species, matrices, flow_rows, flow_columns),
+    )
+
+
+def react_ends(species, matrices, loss, sweeps, to_left, to_right):
+    def body(counts_ref, loss_ref, x_low, a_low, x_high, a_high, l_low, r_low, l_high, r_high, low, high, mats):
+        ends = (low, high)
+
+        def store(p, r, y, result):
+            ends[p][16 * r + y] = result
+
+        react_kernel(
+            [(0, x_low, a_low), (6, x_high, a_high)],
+            range(2), range(2, 14), 16, counts_ref, loss_ref, mats, store,
+        )
+        for target, left_ref, right_ref in ((low, l_low, r_low), (high, l_high, r_high)):
+            for r in range(2):
+                for y in range(2):
+                    target[16 * r + y] = left_ref[2 * r + y]
+                    target[16 * r + 14 + y] = right_ref[2 * r + y]
+
+    edges = [pl.BlockSpec((4, species_count, depth), lambda g, _, b=b: (b, 0, 0)) for b in (0, 3)]
     return react_call(
-        body, f"react_pair_{pair}", 1, 2, lambda g: pair, [edge, edge], [(36, species_count, depth)],
-        (sweeps, species, matrices, loss, to_left, to_right),
-    )[0]
+        body, "react_ends", 1, 2, [lambda g: 0, lambda g: 3], [edges[0], edges[0], edges[1], edges[1]],
+        [(36, species_count, depth)] * 2,
+        (sweeps, loss, species, matrices, species, matrices, to_left, to_right, to_left, to_right),
+    )
 
 
 def react_middle(species, matrices, loss, sweeps):
-    def body(counts_ref, x_ref, a_ref, loss_ref, o_ref, mats):
+    def body(counts_ref, loss_ref, x_ref, a_ref, o_ref, mats):
         g = pl.program_id(0)
 
-        def store(r, y, result):
+        def store(_, r, y, result):
             o_ref[12 * (2 * g + r) + y - 2] = result
 
-        react_kernel(2 + 2 * g, range(2), range(2, 14), 12, counts_ref, x_ref, a_ref, loss_ref, mats, store)
+        react_kernel(
+            [(2 + 2 * g, x_ref, a_ref)], range(2), range(2, 14), 12, counts_ref, loss_ref, mats, store
+        )
 
     return react_call(
-        body, "react_middle", 2, 2, lambda g: 1 + g, [], [(48, species_count, depth)],
-        (sweeps, species, matrices, loss),
+        body, "react_middle", 2, 2, [lambda g: 1 + g], [], [(48, species_count, depth)],
+        (sweeps, loss, species, matrices),
     )[0]
 
 
@@ -408,8 +426,7 @@
     to_left, to_right = react_edges(*kept)
     before = onward(to_right, "gy", 1)
     after = onward(to_left, "gy", -1)
-    high = react_pair(3, *arguments, to_left, to_right)
-    low = react_pair(0, *arguments, to_left, to_right)
+    low, high = react_ends(*arguments, to_left, to_right)
     low, high = add_corners(low, high, before, after, flow_rows, flow_columns)
     above = onward(high, "gx", 1)
     below = onward(low, "gx", -1)

time: 62.3 us -> 61.7 us (level)
  Pallas kernels: 35.8 us -> 32.4 us
  waiting for transfers between devices: 7.88 us -> 11.2 us
    pallas_call x4 -> x3, Pallas kernels: 28.4 us -> 25.1 us  [react_call(): pl.pallas_call(body, out_shape=[jax.ShapeDtypeStruct(s, single) for s in...]
    ppermute x4, waiting for transfers between devices: 7.88 us -> 11.2 us  [onward(): return lax.ppermute(array, axis, pairs)]
  transfers between devices with their start and end apart: 4 -> 4, of which waited for: 2 -> 4; matrix products, arithmetic and copies ran while one was open for 0% -> 0% of each run, Pallas kernels for 36% -> 32%
where the time goes in v3:
time: 61.7 us; the launch traced here: 61.4 us
  Pallas kernels  32.4 us (53%)
  starting transfers between devices  14.3 us (23%)
  waiting for transfers between devices  11.2 us (18%)
  local copies, waits for them, and re-layouts  3.09 us (5%)
    pallas_call x3, Pallas kernels, react_call(): pl.pallas_call(body, out_shape=[jax.ShapeDtypeStruct(s, single) for s in...  25.1 us
    ppermute x4, starting transfers between devices, onward(): return lax.ppermute(array, axis, pairs)  14.3 us
    ppermute x4, waiting for transfers between devices, onward(): return lax.ppermute(array, axis, pairs)  11.2 us
    pallas_call x2, Pallas kernels, moved_call(): pl.pallas_call(body, out_shape=shapes, in_specs=[pl.BlockSpec(memory_spac...  7.02 us
    unnamed x28, local copies, waits for them, and re-layouts  3.09 us
  transfers between devices with their start and end apart: 4, of which 4 were waited for; matrix products, arithmetic and copies ran while one was open for 0% of the time, Pallas kernels for 32%

profile of v3, /device:TPU:198, one launch (start us, length us, event | category | flops | bytes accessed | tf_op | source)
XLA Modules:
  0.0 61.4 jit_solution(1449140023373153337)
XLA Ops:
  0.0 0.0 copy-start.13
  0.0 8.7 %react_edges.1 = (f32[18,48,128]{2,1,0:T(8,128)S(1)}, f32[18,48,128]{2,1,0:T(8,128)S(1)}) custom-call(s32[8,16]{1,0:T(8,128)} %counts_ref.5, f32[1,48]{1,0:T(1,128)} %bitcast.5, f32[48,8,16,128]{3,2,1,0:T(8,128)} %x_ref.3, f32[8,16,2304]{2,1,0:T(8,128)} %a_ref.3, f32[8,16,128]{2,1,0:T(8,128)} %fr_ref.7, f32[8,16,128]{2,1,0:T(8,128)} %fc_ref.7), custom_call_target="tpu_custom_call" | custom-call | tf_op jit(solution)/shard_map/react_edges/pallas_call | solution.py:130
  8.8 0.0 copy-start.2
  8.8 2.7 %collective-permute-start.1 = (f32[18,48,128]{2,1,0:T(8,128)S(1)}, f32[18,48,128]{2,1,0:T(8,128)S(1)}, u32[]{:S(2)}, u32[]{:S(2)}) collective-permute-start(f32[18,48,128]{2,1,0:T(8,128)S(1)} %get-tuple-element.13.l_low.l_high.to_left), channel_id=1, source_target_pairs={{1,0},{2,1},{3,2},{4,3},{5,4},{6,5},{7,6},{9,8},{10,9},{11,10},{12... | collective-permute-start | bytes 1327112 | tf_op jit(solution)/shard_map/ppermute | solution.py:419
  11.5 0.0 copy-start.10
  11.5 0.0 copy-start.11
  11.5 5.4 %collective-permute-start = (f32[18,48,128]{2,1,0:T(8,128)S(1)}, f32[18,48,128]{2,1,0:T(8,128)S(1)}, u32[]{:S(2)}, u32[]{:S(2)}) collective-permute-start(f32[18,48,128]{2,1,0:T(8,128)S(1)} %get-tuple-element.14.r_low.r_high.to_right), channel_id=1, source_target_pairs={{0,1},{1,2},{2,3},{3,4},{4,5},{5,6},{6,7},{8,9},{9,10},{10,11},{11... | collective-permute-start | bytes 1327112 | tf_op jit(solution)/shard_map/ppermute | solution.py:419
  16.9 0.0 copy-done.12
  16.9 0.0 copy-done.1
  16.9 7.6 %react_ends.1 = (f32[36,48,128]{2,1,0:T(8,128)S(1)}, f32[36,48,128]{2,1,0:T(8,128)S(1)}) custom-call(s32[8,16]{1,0:T(8,128)S(1)} %copy-done.12, f32[1,48]{1,0:T(1,128)S(1)} %bitcast.6, f32[48,8,16,128]{3,2,1,0:T(8,128)S(1)} %copy-done, f32[8,16,2304]{2,1,0:T(8,128)S(1)} %copy-done.1, f32[48,8,16,128]{3,2,1,0:T(8,128)S(1)} %copy-done, ...), custom_call_target="tpu_custom_call" | custom-call | tf_op jit(solution)/shard_map/react_ends/pallas_call | solution.py:130
  24.5 0.1 collective-permute-done.1.after
  24.7 1.3 %collective-permute-done.before = f32[18,48,128]{2,1,0:T(8,128)S(1)} collective-permute-done((f32[18,48,128]{2,1,0:T(8,128)S(1)}, f32[18,48,128]{2,1,0:T(8,128)S(1)}, u32[]{:S(2)}, u32[]{:S(2)}) %collective-permute-start) | collective-permute-done | bytes 442400 | tf_op jit(solution)/shard_map/ppermute | solution.py:419
  26.0 0.3 add_corners.1
  26.3 4.1 %collective-permute-start.3 = (f32[36,48,128]{2,1,0:T(8,128)S(1)}, f32[36,48,128]{2,1,0:T(8,128)}, u32[]{:S(2)}, u32[]{:S(2)}) collective-permute-start(f32[36,48,128]{2,1,0:T(8,128)S(1)} %get-tuple-element.17.low), channel_id=1, source_target_pairs={{8,0},{16,8},{24,16},{32,24},{40,32},{48,40},{56,48},{64,56},{72,6... | collective-permute-start | bytes 2654216 | tf_op jit(solution)/shard_map/ppermute | solution.py:419
  30.4 2.1 %collective-permute-start.2 = (f32[36,48,128]{2,1,0:T(8,128)S(1)}, f32[36,48,128]{2,1,0:T(8,128)}, u32[]{:S(2)}, u32[]{:S(2)}) collective-permute-start(f32[36,48,128]{2,1,0:T(8,128)S(1)} %get-tuple-element.18.high), channel_id=1, source_target_pairs={{0,8},{8,16},{16,24},{24,32},{32,40},{40,48},{48,56},{56,64},{64,7... | collective-permute-start | bytes 2654216 | tf_op jit(solution)/shard_map/ppermute | solution.py:419
  32.6 8.7 %react_middle.1.middle = f32[48,48,128]{2,1,0:T(8,128)S(1)} custom-call(s32[8,16]{1,0:T(8,128)S(1)} %copy-done.12, f32[1,48]{1,0:T(1,128)S(1)} %bitcast.7, f32[48,8,16,128]{3,2,1,0:T(8,128)S(1)} %copy-done, f32[8,16,2304]{2,1,0:T(8,128)S(1)} %copy-done.1), custom_call_target="tpu_custom_call" | custom-call | tf_op jit(solution)/shard_map/react_middle/pallas_call | solution.py:130
  41.3 0.1 add_convert_fusion.inside_ref
  41.4 1.0 %copy-done.3 = f32[18,48,128]{2,1,0:T(8,128)S(1)} copy-done((f32[18,48,128]{2,1,0:T(8,128)S(1)}, f32[18,48,128]{2,1,0:T(8,128)}, u32[]{:S(2)}) %copy-start.3) | copy-done | bytes 442392
  42.4 1.0 %copy-done.5 = f32[18,48,128]{2,1,0:T(8,128)S(1)} copy-done((f32[18,48,128]{2,1,0:T(8,128)S(1)}, f32[18,48,128]{2,1,0:T(8,128)}, u32[]{:S(2)}) %copy-start.5) | copy-done | bytes 442392
  43.4 1.0 %copy-done.8 = f32[18,48,128]{2,1,0:T(8,128)S(1)} copy-done((f32[18,48,128]{2,1,0:T(8,128)S(1)}, f32[18,48,128]{2,1,0:T(8,128)}, u32[]{:S(2)}) %copy-start.8) | copy-done | bytes 442392
  44.4 3.2 %inner.1 = (f32[48,8,16,128]{3,2,1,0:T(8,128)}, f32[6,18,48,128]{3,2,1,0:T(8,128)S(1)}) custom-call(s32[4]{0:T(128)S(1)} %add_convert_fusion.inside_ref, f32[36,48,128]{2,1,0:T(8,128)S(1)} %get-tuple-element.17.low, f32[48,48,128]{2,1,0:T(8,128)S(1)} %react_middle.1.middle, f32[36,48,128]{2,1,0:T(8,128)S(1)} %get-tuple-element.18.high, ...), custom_call_target="tpu_custom_call" | custom-call | tf_op jit(solution)/shard_map/inner/pallas_call | solution.py:379
  47.6 2.5 %collective-permute-done.3.below = f32[36,48,128]{2,1,0:T(8,128)} collective-permute-done((f32[36,48,128]{2,1,0:T(8,128)S(1)}, f32[36,48,128]{2,1,0:T(8,128)}, u32[]{:S(2)}, u32[]{:S(2)}) %collective-permute-start.3) | collective-permute-done | bytes 884768 | tf_op jit(solution)/shard_map/ppermute | solution.py:419
  50.1 7.3 %collective-permute-done.2.above = f32[36,48,128]{2,1,0:T(8,128)} collective-permute-done((f32[36,48,128]{2,1,0:T(8,128)S(1)}, f32[36,48,128]{2,1,0:T(8,128)}, u32[]{:S(2)}, u32[]{:S(2)}) %collective-permute-start.2) | collective-permute-done | bytes 884768 | tf_op jit(solution)/shard_map/ppermute | solution.py:419
  57.4 3.8 %outer.1 = f32[48,8,16,128]{3,2,1,0:T(8,128)} custom-call(s32[4]{0:T(128)S(1)} %add_convert_fusion.inside_ref, f32[48,8,16,128]{3,2,1,0:T(8,128)} %get-tuple-element.19.done, f32[6,18,48,128]{3,2,1,0:T(8,128)S(1)} %get-tuple-element.20.inner, f32[36,48,128]{2,1,0:T(8,128)S(1)} %get-tuple-element.17.low, ...), custom_call_target="tpu_custom_call", output_to_operand_aliasing={{}: (1, {})} | custom-call | tf_op jit(solution)/shard_map/outer/pallas_call | solution.py:379
  (19 shorter events, 0.0 us)
Async XLA Ops:
  0.0 16.9 %copy-start.12 = (s32[8,16]{1,0:T(8,128)S(1)}, s32[8,16]{1,0:T(8,128)}, u32[]{:S(2)}) copy-start(s32[8,16]{1,0:T(8,128)} %counts_ref.5) | copy-start | bytes 1540
  0.0 16.9 %copy-start.1 = (f32[8,16,2304]{2,1,0:T(8,128)S(1)}, f32[8,16,2304]{2,1,0:T(8,128)}, u32[]{:S(2)}) copy-start(f32[8,16,2304]{2,1,0:T(8,128)} %a_ref.3) | copy-start | bytes 3538948
  0.0 16.9 %copy-start = (f32[48,8,16,128]{3,2,1,0:T(8,128)S(1)}, f32[48,8,16,128]{3,2,1,0:T(8,128)}, u32[]{:S(2)}) copy-start(f32[48,8,16,128]{3,2,1,0:T(8,128)} %x_ref.3) | copy-start | bytes 9437188
  0.0 16.9 %copy-start.13 = (f32[48]{0:T(128)S(1)}, f32[48]{0:T(128)}, u32[]{:S(2)}) copy-start(f32[48]{0:T(128)} %param.8) | copy-start | bytes 580
  8.8 15.8 %copy-start.2 = (f32[18,48,128]{2,1,0:T(8,128)}, f32[18,48,128]{2,1,0:T(8,128)S(1)}, u32[]{:S(2)}) copy-start(f32[18,48,128]{2,1,0:T(8,128)S(1)} %get-tuple-element.14.r_low.r_high.to_right) | copy-start | bytes 1327108
  8.8 15.9 %collective-permute-start.1 = (f32[18,48,128]{2,1,0:T(8,128)S(1)}, f32[18,48,128]{2,1,0:T(8,128)S(1)}, u32[]{:S(2)}, u32[]{:S(2)}) collective-permute-start(f32[18,48,128]{2,1,0:T(8,128)S(1)} %get-tuple-element.13.l_low.l_high.to_left), channel_id=1, source_target_pairs={{1,0},{2,1},{3,2},{4,3},{5,4},{6,5},{7,6},{9,8},{10,9},{11,10},{12... | collective-permute-start | bytes 1327112 | tf_op jit(solution)/shard_map/ppermute | solution.py:419
  11.5 14.5 %copy-start.10 = (f32[8,16,128]{2,1,0:T(8,128)S(1)}, f32[8,16,128]{2,1,0:T(8,128)}, u32[]{:S(2)}) copy-start(f32[8,16,128]{2,1,0:T(8,128)} %fr_ref.7) | copy-start | bytes 196612
  11.5 14.5 %copy-start.11 = (f32[8,16,128]{2,1,0:T(8,128)S(1)}, f32[8,16,128]{2,1,0:T(8,128)}, u32[]{:S(2)}) copy-start(f32[8,16,128]{2,1,0:T(8,128)} %fc_ref.7) | copy-start | bytes 196612
  11.5 14.5 %collective-permute-start = (f32[18,48,128]{2,1,0:T(8,128)S(1)}, f32[18,48,128]{2,1,0:T(8,128)S(1)}, u32[]{:S(2)}, u32[]{:S(2)}) collective-permute-start(f32[18,48,128]{2,1,0:T(8,128)S(1)} %get-tuple-element.14.r_low.r_high.to_right), channel_id=1, source_target_pairs={{0,1},{1,2},{2,3},{3,4},{4,5},{5,6},{6,7},{8,9},{9,10},{10,11},{11... | collective-permute-start | bytes 1327112 | tf_op jit(solution)/shard_map/ppermute | solution.py:419
  24.7 7.9 %copy-start.4 = (f32[18,48,128]{2,1,0:T(8,128)}, f32[18,48,128]{2,1,0:T(8,128)S(1)}, u32[]{:S(2)}) copy-start(f32[18,48,128]{2,1,0:T(8,128)S(1)} %collective-permute-done.1.after) | copy-start | bytes 1327108
  26.0 6.5 %copy-start.7 = (f32[18,48,128]{2,1,0:T(8,128)}, f32[18,48,128]{2,1,0:T(8,128)S(1)}, u32[]{:S(2)}) copy-start(f32[18,48,128]{2,1,0:T(8,128)S(1)} %collective-permute-done.before) | copy-start | bytes 1327108
  26.3 23.7 %collective-permute-start.3 = (f32[36,48,128]{2,1,0:T(8,128)S(1)}, f32[36,48,128]{2,1,0:T(8,128)}, u32[]{:S(2)}, u32[]{:S(2)}) collective-permute-start(f32[36,48,128]{2,1,0:T(8,128)S(1)} %get-tuple-element.17.low), channel_id=1, source_target_pairs={{8,0},{16,8},{24,16},{32,24},{40,32},{48,40},{56,48},{64,56},{72,6... | collective-permute-start | bytes 2654216 | tf_op jit(solution)/shard_map/ppermute | solution.py:419
  30.4 27.0 %collective-permute-start.2 = (f32[36,48,128]{2,1,0:T(8,128)S(1)}, f32[36,48,128]{2,1,0:T(8,128)}, u32[]{:S(2)}, u32[]{:S(2)}) collective-permute-start(f32[36,48,128]{2,1,0:T(8,128)S(1)} %get-tuple-element.18.high), channel_id=1, source_target_pairs={{0,8},{8,16},{16,24},{24,32},{32,40},{40,48},{48,56},{56,64},{64,7... | collective-permute-start | bytes 2654216 | tf_op jit(solution)/shard_map/ppermute | solution.py:419
  41.4 1.0 %copy-start.3 = (f32[18,48,128]{2,1,0:T(8,128)S(1)}, f32[18,48,128]{2,1,0:T(8,128)}, u32[]{:S(2)}) copy-start(f32[18,48,128]{2,1,0:T(8,128)} %copy-done.2) | copy-start | bytes 1327108
  42.4 1.0 %copy-start.5 = (f32[18,48,128]{2,1,0:T(8,128)S(1)}, f32[18,48,128]{2,1,0:T(8,128)}, u32[]{:S(2)}) copy-start(f32[18,48,128]{2,1,0:T(8,128)} %copy-done.4) | copy-start | bytes 1327108
  43.4 1.0 %copy-start.8 = (f32[18,48,128]{2,1,0:T(8,128)S(1)}, f32[18,48,128]{2,1,0:T(8,128)}, u32[]{:S(2)}) copy-start(f32[18,48,128]{2,1,0:T(8,128)} %copy-done.7) | copy-start | bytes 1327108
  44.4 12.9 %copy-start.6 = (f32[18,48,128]{2,1,0:T(8,128)S(1)}, f32[18,48,128]{2,1,0:T(8,128)}, u32[]{:S(2)}) copy-start(f32[18,48,128]{2,1,0:T(8,128)} %copy-done.4) | copy-start | bytes 1327108
  44.4 12.9 %copy-start.9 = (f32[18,48,128]{2,1,0:T(8,128)S(1)}, f32[18,48,128]{2,1,0:T(8,128)}, u32[]{:S(2)}) copy-start(f32[18,48,128]{2,1,0:T(8,128)} %copy-done.7) | copy-start | bytes 1327108

commit v4 on v3

--- a/solution.py
+++ b/solution.py
@@ -46,8 +46,9 @@
         inverse.append(1.0 / scaled)
         one.append((gamma * (matrix - matrix * eye)) * inverse[c])
         left_one.append(left(one[c]))
-    two = [times(left_one[c], right(one[c])) for c in every]
-    base = [times(left_one[c], right(loads[c]())) for c in every]
+    both = [times(left_one[c], right(jnp.concatenate([loads[c](), one[c]], axis=1))) for c in every]
+    two = [pair[:, depth:] for pair in both]
+    base = [pair[:, :depth] for pair in both]
     left_two = [left(two[c]) for c in every]
     pair = [times(left_two[c], right(one[c] + pltpu.roll(two[c], 64, 1))) for c in every]
     three = [jnp.where(lane < species_count, pair[c], 0.0) for c in every]

time: 61.7 us -> 61.6 us (level)
  waiting for transfers between devices: 11.2 us -> 9.08 us
  Pallas kernels: 32.4 us -> 33.7 us
    ppermute x4, waiting for transfers between devices: 11.2 us -> 9.08 us  [onward(): return lax.ppermute(array, axis, pairs)]
    pallas_call x3, Pallas kernels: 25.1 us -> 26.3 us  [react_call(): pl.pallas_call(body, out_shape=[jax.ShapeDtypeStruct(s, single) for s in...]
    ppermute x4, starting transfers between devices: 14.3 us -> 14.9 us  [onward(): return lax.ppermute(array, axis, pairs)]
  transfers between devices with their start and end apart: 4 -> 4, of which waited for: 4 -> 2; matrix products, arithmetic and copies ran while one was open for 0% -> 0% of each run, Pallas kernels for 32% -> 34%
where the time goes in v4:
time: 61.6 us; the launch traced here: 61.2 us
  Pallas kernels  33.7 us (55%)
  starting transfers between devices  14.9 us (24%)
  waiting for transfers between devices  9.08 us (15%)
  local copies, waits for them, and re-layouts  3.09 us (5%)
    pallas_call x3, Pallas kernels, react_call(): pl.pallas_call(body, out_shape=[jax.ShapeDtypeStruct(s, single) for s in...  26.3 us
    ppermute x4, starting transfers between devices, onward(): return lax.ppermute(array, axis, pairs)  14.9 us
    ppermute x4, waiting for transfers between devices, onward(): return lax.ppermute(array, axis, pairs)  9.08 us
    pallas_call x2, Pallas kernels, moved_call(): pl.pallas_call(body, out_shape=shapes, in_specs=[pl.BlockSpec(memory_spac...  7.02 us
    unnamed x28, local copies, waits for them, and re-layouts  3.09 us
  transfers between devices with their start and end apart: 4, of which 2 were waited for; matrix products, arithmetic and copies ran while one was open for 0% of the time, Pallas kernels for 34%

profile of v4, /device:TPU:198, one launch (start us, length us, event | category | flops | bytes accessed | tf_op | source)
XLA Modules:
  0.0 61.2 jit_solution(4422015764057481104)
XLA Ops:
  0.0 0.0 copy-start.13
  0.0 8.6 %react_edges.1 = (f32[18,48,128]{2,1,0:T(8,128)S(1)}, f32[18,48,128]{2,1,0:T(8,128)S(1)}) custom-call(s32[8,16]{1,0:T(8,128)} %counts_ref.5, f32[1,48]{1,0:T(1,128)} %bitcast.5, f32[48,8,16,128]{3,2,1,0:T(8,128)} %x_ref.3, f32[8,16,2304]{2,1,0:T(8,128)} %a_ref.3, f32[8,16,128]{2,1,0:T(8,128)} %fr_ref.7, f32[8,16,128]{2,1,0:T(8,128)} %fc_ref.7), custom_call_target="tpu_custom_call" | custom-call | tf_op jit(solution)/shard_map/react_edges/pallas_call | solution.py:131
  8.6 0.0 copy-start.2
  8.6 2.7 %collective-permute-start.1 = (f32[18,48,128]{2,1,0:T(8,128)S(1)}, f32[18,48,128]{2,1,0:T(8,128)S(1)}, u32[]{:S(2)}, u32[]{:S(2)}) collective-permute-start(f32[18,48,128]{2,1,0:T(8,128)S(1)} %get-tuple-element.13.l_low.l_high.to_left), channel_id=1, source_target_pairs={{1,0},{2,1},{3,2},{4,3},{5,4},{6,5},{7,6},{9,8},{10,9},{11,10},{12... | collective-permute-start | bytes 1327112 | tf_op jit(solution)/shard_map/ppermute | solution.py:420
  11.3 0.0 copy-start.10
  11.3 0.0 copy-start.11
  11.4 5.3 %collective-permute-start = (f32[18,48,128]{2,1,0:T(8,128)S(1)}, f32[18,48,128]{2,1,0:T(8,128)S(1)}, u32[]{:S(2)}, u32[]{:S(2)}) collective-permute-start(f32[18,48,128]{2,1,0:T(8,128)S(1)} %get-tuple-element.14.r_low.r_high.to_right), channel_id=1, source_target_pairs={{0,1},{1,2},{2,3},{3,4},{4,5},{5,6},{6,7},{8,9},{9,10},{10,11},{11... | collective-permute-start | bytes 1327112 | tf_op jit(solution)/shard_map/ppermute | solution.py:420
  16.8 9.3 %react_ends.1 = (f32[36,48,128]{2,1,0:T(8,128)S(1)}, f32[36,48,128]{2,1,0:T(8,128)S(1)}) custom-call(s32[8,16]{1,0:T(8,128)S(1)} %copy-done.12, f32[1,48]{1,0:T(1,128)S(1)} %bitcast.6, f32[48,8,16,128]{3,2,1,0:T(8,128)S(1)} %copy-done, f32[8,16,2304]{2,1,0:T(8,128)S(1)} %copy-done.1, f32[48,8,16,128]{3,2,1,0:T(8,128)S(1)} %copy-done, ...), custom_call_target="tpu_custom_call" | custom-call | tf_op jit(solution)/shard_map/react_ends/pallas_call | solution.py:131
  26.1 0.0 copy-done.2
  26.1 0.0 collective-permute-done.1.after
  26.1 0.0 collective-permute-done.before
  26.1 0.3 add_corners.1
  26.5 4.7 %collective-permute-start.3 = (f32[36,48,128]{2,1,0:T(8,128)S(1)}, f32[36,48,128]{2,1,0:T(8,128)}, u32[]{:S(2)}, u32[]{:S(2)}) collective-permute-start(f32[36,48,128]{2,1,0:T(8,128)S(1)} %get-tuple-element.17.low), channel_id=1, source_target_pairs={{8,0},{16,8},{24,16},{32,24},{40,32},{48,40},{56,48},{64,56},{72,6... | collective-permute-start | bytes 2654216 | tf_op jit(solution)/shard_map/ppermute | solution.py:420
  31.2 2.1 %collective-permute-start.2 = (f32[36,48,128]{2,1,0:T(8,128)S(1)}, f32[36,48,128]{2,1,0:T(8,128)}, u32[]{:S(2)}, u32[]{:S(2)}) collective-permute-start(f32[36,48,128]{2,1,0:T(8,128)S(1)} %get-tuple-element.18.high), channel_id=1, source_target_pairs={{0,8},{8,16},{16,24},{24,32},{32,40},{40,48},{48,56},{56,64},{64,7... | collective-permute-start | bytes 2654216 | tf_op jit(solution)/shard_map/ppermute | solution.py:420
  33.3 0.0 copy-done.7
  33.3 8.5 %react_middle.1.middle = f32[48,48,128]{2,1,0:T(8,128)S(1)} custom-call(s32[8,16]{1,0:T(8,128)S(1)} %copy-done.12, f32[1,48]{1,0:T(1,128)S(1)} %bitcast.7, f32[48,8,16,128]{3,2,1,0:T(8,128)S(1)} %copy-done, f32[8,16,2304]{2,1,0:T(8,128)S(1)} %copy-done.1), custom_call_target="tpu_custom_call" | custom-call | tf_op jit(solution)/shard_map/react_middle/pallas_call | solution.py:131
  41.8 0.1 add_convert_fusion.inside_ref
  41.9 1.0 %copy-done.3 = f32[18,48,128]{2,1,0:T(8,128)S(1)} copy-done((f32[18,48,128]{2,1,0:T(8,128)S(1)}, f32[18,48,128]{2,1,0:T(8,128)}, u32[]{:S(2)}) %copy-start.3) | copy-done | bytes 442392
  42.9 1.0 %copy-done.5 = f32[18,48,128]{2,1,0:T(8,128)S(1)} copy-done((f32[18,48,128]{2,1,0:T(8,128)S(1)}, f32[18,48,128]{2,1,0:T(8,128)}, u32[]{:S(2)}) %copy-start.5) | copy-done | bytes 442392
  43.9 1.0 %copy-done.8 = f32[18,48,128]{2,1,0:T(8,128)S(1)} copy-done((f32[18,48,128]{2,1,0:T(8,128)S(1)}, f32[18,48,128]{2,1,0:T(8,128)}, u32[]{:S(2)}) %copy-start.8) | copy-done | bytes 442392
  44.9 3.2 %inner.1 = (f32[48,8,16,128]{3,2,1,0:T(8,128)}, f32[6,18,48,128]{3,2,1,0:T(8,128)S(1)}) custom-call(s32[4]{0:T(128)S(1)} %add_convert_fusion.inside_ref, f32[36,48,128]{2,1,0:T(8,128)S(1)} %get-tuple-element.17.low, f32[48,48,128]{2,1,0:T(8,128)S(1)} %react_middle.1.middle, f32[36,48,128]{2,1,0:T(8,128)S(1)} %get-tuple-element.18.high, ...), custom_call_target="tpu_custom_call" | custom-call | tf_op jit(solution)/shard_map/inner/pallas_call | solution.py:380
  48.1 1.8 %collective-permute-done.3.below = f32[36,48,128]{2,1,0:T(8,128)} collective-permute-done((f32[36,48,128]{2,1,0:T(8,128)S(1)}, f32[36,48,128]{2,1,0:T(8,128)}, u32[]{:S(2)}, u32[]{:S(2)}) %collective-permute-start.3) | collective-permute-done | bytes 884768 | tf_op jit(solution)/shard_map/ppermute | solution.py:420
  49.9 7.2 %collective-permute-done.2.above = f32[36,48,128]{2,1,0:T(8,128)} collective-permute-done((f32[36,48,128]{2,1,0:T(8,128)S(1)}, f32[36,48,128]{2,1,0:T(8,128)}, u32[]{:S(2)}, u32[]{:S(2)}) %collective-permute-start.2) | collective-permute-done | bytes 884768 | tf_op jit(solution)/shard_map/ppermute | solution.py:420
  57.2 3.8 %outer.1 = f32[48,8,16,128]{3,2,1,0:T(8,128)} custom-call(s32[4]{0:T(128)S(1)} %add_convert_fusion.inside_ref, f32[48,8,16,128]{3,2,1,0:T(8,128)} %get-tuple-element.19.done, f32[6,18,48,128]{3,2,1,0:T(8,128)S(1)} %get-tuple-element.20.inner, f32[36,48,128]{2,1,0:T(8,128)S(1)} %get-tuple-element.17.low, ...), custom_call_target="tpu_custom_call", output_to_operand_aliasing={{}: (1, {})} | custom-call | tf_op jit(solution)/shard_map/outer/pallas_call | solution.py:380
  (19 shorter events, 0.0 us)
Async XLA Ops:
  0.0 16.7 %copy-start.12 = (s32[8,16]{1,0:T(8,128)S(1)}, s32[8,16]{1,0:T(8,128)}, u32[]{:S(2)}) copy-start(s32[8,16]{1,0:T(8,128)} %counts_ref.5) | copy-start | bytes 1540
  0.0 16.7 %copy-start.1 = (f32[8,16,2304]{2,1,0:T(8,128)S(1)}, f32[8,16,2304]{2,1,0:T(8,128)}, u32[]{:S(2)}) copy-start(f32[8,16,2304]{2,1,0:T(8,128)} %a_ref.3) | copy-start | bytes 3538948
  0.0 16.7 %copy-start = (f32[48,8,16,128]{3,2,1,0:T(8,128)S(1)}, f32[48,8,16,128]{3,2,1,0:T(8,128)}, u32[]{:S(2)}) copy-start(f32[48,8,16,128]{3,2,1,0:T(8,128)} %x_ref.3) | copy-start | bytes 9437188
  0.0 16.7 %copy-start.13 = (f32[48]{0:T(128)S(1)}, f32[48]{0:T(128)}, u32[]{:S(2)}) copy-start(f32[48]{0:T(128)} %param.8) | copy-start | bytes 580
  8.6 17.5 %copy-start.2 = (f32[18,48,128]{2,1,0:T(8,128)}, f32[18,48,128]{2,1,0:T(8,128)S(1)}, u32[]{:S(2)}) copy-start(f32[18,48,128]{2,1,0:T(8,128)S(1)} %get-tuple-element.14.r_low.r_high.to_right) | copy-start | bytes 1327108
  8.6 17.5 %collective-permute-start.1 = (f32[18,48,128]{2,1,0:T(8,128)S(1)}, f32[18,48,128]{2,1,0:T(8,128)S(1)}, u32[]{:S(2)}, u32[]{:S(2)}) collective-permute-start(f32[18,48,128]{2,1,0:T(8,128)S(1)} %get-tuple-element.13.l_low.l_high.to_left), channel_id=1, source_target_pairs={{1,0},{2,1},{3,2},{4,3},{5,4},{6,5},{7,6},{9,8},{10,9},{11,10},{12... | collective-permute-start | bytes 1327112 | tf_op jit(solution)/shard_map/ppermute | solution.py:420
  11.3 14.8 %copy-start.10 = (f32[8,16,128]{2,1,0:T(8,128)S(1)}, f32[8,16,128]{2,1,0:T(8,128)}, u32[]{:S(2)}) copy-start(f32[8,16,128]{2,1,0:T(8,128)} %fr_ref.7) | copy-start | bytes 196612
  11.3 14.8 %copy-start.11 = (f32[8,16,128]{2,1,0:T(8,128)S(1)}, f32[8,16,128]{2,1,0:T(8,128)}, u32[]{:S(2)}) copy-start(f32[8,16,128]{2,1,0:T(8,128)} %fc_ref.7) | copy-start | bytes 196612
  11.4 14.7 %collective-permute-start = (f32[18,48,128]{2,1,0:T(8,128)S(1)}, f32[18,48,128]{2,1,0:T(8,128)S(1)}, u32[]{:S(2)}, u32[]{:S(2)}) collective-permute-start(f32[18,48,128]{2,1,0:T(8,128)S(1)} %get-tuple-element.14.r_low.r_high.to_right), channel_id=1, source_target_pairs={{0,1},{1,2},{2,3},{3,4},{4,5},{5,6},{6,7},{8,9},{9,10},{10,11},{11... | collective-permute-start | bytes 1327112 | tf_op jit(solution)/shard_map/ppermute | solution.py:420
  26.1 7.2 %copy-start.4 = (f32[18,48,128]{2,1,0:T(8,128)}, f32[18,48,128]{2,1,0:T(8,128)S(1)}, u32[]{:S(2)}) copy-start(f32[18,48,128]{2,1,0:T(8,128)S(1)} %collective-permute-done.1.after) | copy-start | bytes 1327108
  26.1 7.2 %copy-start.7 = (f32[18,48,128]{2,1,0:T(8,128)}, f32[18,48,128]{2,1,0:T(8,128)S(1)}, u32[]{:S(2)}) copy-start(f32[18,48,128]{2,1,0:T(8,128)S(1)} %collective-permute-done.before) | copy-start | bytes 1327108
  26.5 23.5 %collective-permute-start.3 = (f32[36,48,128]{2,1,0:T(8,128)S(1)}, f32[36,48,128]{2,1,0:T(8,128)}, u32[]{:S(2)}, u32[]{:S(2)}) collective-permute-start(f32[36,48,128]{2,1,0:T(8,128)S(1)} %get-tuple-element.17.low), channel_id=1, source_target_pairs={{8,0},{16,8},{24,16},{32,24},{40,32},{48,40},{56,48},{64,56},{72,6... | collective-permute-start | bytes 2654216 | tf_op jit(solution)/shard_map/ppermute | solution.py:420
  31.2 26.0 %collective-permute-start.2 = (f32[36,48,128]{2,1,0:T(8,128)S(1)}, f32[36,48,128]{2,1,0:T(8,128)}, u32[]{:S(2)}, u32[]{:S(2)}) collective-permute-start(f32[36,48,128]{2,1,0:T(8,128)S(1)} %get-tuple-element.18.high), channel_id=1, source_target_pairs={{0,8},{8,16},{16,24},{24,32},{32,40},{40,48},{48,56},{56,64},{64,7... | collective-permute-start | bytes 2654216 | tf_op jit(solution)/shard_map/ppermute | solution.py:420
  41.9 1.0 %copy-start.3 = (f32[18,48,128]{2,1,0:T(8,128)S(1)}, f32[18,48,128]{2,1,0:T(8,128)}, u32[]{:S(2)}) copy-start(f32[18,48,128]{2,1,0:T(8,128)} %copy-done.2) | copy-start | bytes 1327108
  42.9 1.0 %copy-start.5 = (f32[18,48,128]{2,1,0:T(8,128)S(1)}, f32[18,48,128]{2,1,0:T(8,128)}, u32[]{:S(2)}) copy-start(f32[18,48,128]{2,1,0:T(8,128)} %copy-done.4) | copy-start | bytes 1327108
  43.9 1.0 %copy-start.8 = (f32[18,48,128]{2,1,0:T(8,128)S(1)}, f32[18,48,128]{2,1,0:T(8,128)}, u32[]{:S(2)}) copy-start(f32[18,48,128]{2,1,0:T(8,128)} %copy-done.7) | copy-start | bytes 1327108
  44.9 12.3 %copy-start.6 = (f32[18,48,128]{2,1,0:T(8,128)S(1)}, f32[18,48,128]{2,1,0:T(8,128)}, u32[]{:S(2)}) copy-start(f32[18,48,128]{2,1,0:T(8,128)} %copy-done.4) | copy-start | bytes 1327108
  44.9 12.3 %copy-start.9 = (f32[18,48,128]{2,1,0:T(8,128)S(1)}, f32[18,48,128]{2,1,0:T(8,128)}, u32[]{:S(2)}) copy-start(f32[18,48,128]{2,1,0:T(8,128)} %copy-done.7) | copy-start | bytes 1327108
